TPU v7x, 32 devices: a whole 2x2x4 slice. The times are simulated.
32 devices in a mesh: dp: 8 (over z, y), tensor: 4 (over x, core).
Axes of the slice: x: 2, y: 2, z: 4, core: 2. Of those that a mesh axis runs over, the one named last changes fastest.
Arguments:
- inputs: bfloat16 [16, 1024, 512], P('dp', 'tensor'), may hold values from -6 to 6
- memory: bfloat16 [16, 1024, 512], P('dp', 'tensor'), may hold values from -6 to 6
- tgt_len: int32 [16], P('dp'), may hold values from 512 to 1024, as said below
- src_len: int32 [16], P('dp'), may hold values from 512 to 1024, as said below
- cotangent: bfloat16 [16, 1024, 512], P('dp', 'tensor'), may hold values from -6 to 6
- w_qkv: bfloat16 [3, 512, 512], P(None, 'dp', 'tensor'), may hold values from -0.25 to 0.25
- w_out: bfloat16 [512, 512], P('tensor', 'dp'), may hold values from -6 to 6
- cross_query: bfloat16 [512, 512], P('dp', 'tensor'), may hold values from -0.25 to 0.25
- cross_kv: bfloat16 [2, 512, 512], P(None, 'dp', 'tensor'), may hold values from -0.25 to 0.25
- cross_out: bfloat16 [512, 512], P('tensor', 'dp'), may hold values from -6 to 6
- ffn_up: bfloat16 [512, 2048], P('dp', 'tensor'), may hold values from -0.25 to 0.25
- ffn_down: bfloat16 [2048, 512], P('tensor', 'dp'), may hold values from -0.1875 to 0.1875
- gain_one: bfloat16 [512], P('dp'), may hold values from 0.099609375 to 1.8984375
- bias_one: bfloat16 [512], P('dp'), may hold values from -3 to 3
- gain_two: bfloat16 [512], P('dp'), may hold values from 0.099609375 to 1.8984375
- bias_two: bfloat16 [512], P('dp'), may hold values from -3 to 3
- gain_three: bfloat16 [512], P('dp'), may hold values from 0.099609375 to 1.8984375
- bias_three: bfloat16 [512], P('dp'), may hold values from -3 to 3
Outputs:
- output: bfloat16 [16, 1024, 512], P('dp', 'tensor')
- grad_inputs: float32 [16, 1024, 512], P('dp', 'tensor')
- grad_memory: float32 [16, 1024, 512], P('dp', 'tensor')
- grad_w_qkv: float32 [3, 512, 512], P(None, 'dp', 'tensor')
- grad_w_out: float32 [512, 512], P('tensor', 'dp')
- grad_cross_query: float32 [512, 512], P('dp', 'tensor')
- grad_cross_kv: float32 [2, 512, 512], P(None, 'dp', 'tensor')
- grad_cross_out: float32 [512, 512], P('tensor', 'dp')
- grad_ffn_up: float32 [512, 2048], P('dp', 'tensor')
- grad_ffn_down: float32 [2048, 512], P('tensor', 'dp')
- grad_gain_one: float32 [512], P('dp')
- grad_bias_one: float32 [512], P('dp')
- grad_gain_two: float32 [512], P('dp')
- grad_bias_two: float32 [512], P('dp')
- grad_gain_three: float32 [512], P('dp')
- grad_bias_three: float32 [512], P('dp')
Inputs may be any that keep to these rules, and one draw needn't show every extreme that they name: `tgt_len`: one sequence has a target length of 1024 and another of 512. `src_len`: one sequence has a source length of 1024 and another of 512.
All inputs are finite; a program needn't handle non-finite values.
Results may differ from a plain program's by a relative error of at most 0.015.
Values may be sent and summed in bfloat16 or wider, within the bound.
A program may use at most 128 MiB of HBM per device.

v0:
```python
import jax
import jax.numpy as jnp
from jax import lax
from jax.sharding import PartitionSpec as P

DH = 64
EPSILON = 1e-05
MASKED = -1e30
BLOCK_ROWS = 512


def layer_norm(values, gain_vec, bias_vec):
    center = values - jnp.mean(values, axis=-1, keepdims=True)
    spread = jnp.mean(center * center, axis=-1, keepdims=True)
    return center * lax.rsqrt(spread + EPSILON) * gain_vec + bias_vec


def smooth_gate(values):
    return jax.nn.gelu(values, approximate=True)


def gather_weights(
    w_qkv,
    w_out,
    cross_query,
    cross_kv,
    cross_out,
    ffn_up,
    ffn_down,
    gain_one,
    bias_one,
    gain_two,
    bias_two,
    gain_three,
    bias_three,
):
    return (
        lax.all_gather(w_qkv, "dp", axis=1, tiled=True),
        lax.all_gather(w_out, "dp", axis=1, tiled=True),
        lax.all_gather(cross_query, "dp", axis=0, tiled=True),
        lax.all_gather(cross_kv, "dp", axis=1, tiled=True),
        lax.all_gather(cross_out, "dp", axis=1, tiled=True),
        lax.all_gather(ffn_up, "dp", axis=0, tiled=True),
        lax.all_gather(ffn_down, "dp", axis=1, tiled=True),
        lax.all_gather(gain_one, "dp", axis=0, tiled=True),
        lax.all_gather(bias_one, "dp", axis=0, tiled=True),
        lax.all_gather(gain_two, "dp", axis=0, tiled=True),
        lax.all_gather(bias_two, "dp", axis=0, tiled=True),
        lax.all_gather(gain_three, "dp", axis=0, tiled=True),
        lax.all_gather(bias_three, "dp", axis=0, tiled=True),
    )


def reduce_grads(
    grad_qkv,
    grad_out,
    grad_query,
    grad_pair,
    grad_cross,
    grad_up,
    grad_down,
    grad_gain_one,
    grad_bias_one,
    grad_gain_two,
    grad_bias_two,
    grad_gain_three,
    grad_bias_three,
):
    return (
        lax.psum_scatter(grad_qkv, "dp", scatter_dimension=1, tiled=True),
        lax.psum_scatter(grad_out, "dp", scatter_dimension=1, tiled=True),
        lax.psum_scatter(grad_query, "dp", scatter_dimension=0, tiled=True),
        lax.psum_scatter(grad_pair, "dp", scatter_dimension=1, tiled=True),
        lax.psum_scatter(grad_cross, "dp", scatter_dimension=1, tiled=True),
        lax.psum_scatter(grad_up, "dp", scatter_dimension=0, tiled=True),
        lax.psum_scatter(grad_down, "dp", scatter_dimension=1, tiled=True),
        lax.psum_scatter(grad_gain_one, "dp", scatter_dimension=0, tiled=True),
        lax.psum_scatter(grad_bias_one, "dp", scatter_dimension=0, tiled=True),
        lax.psum_scatter(grad_gain_two, "dp", scatter_dimension=0, tiled=True),
        lax.psum_scatter(grad_bias_two, "dp", scatter_dimension=0, tiled=True),
        lax.psum_scatter(grad_gain_three, "dp", scatter_dimension=0, tiled=True),
        lax.psum_scatter(grad_bias_three, "dp", scatter_dimension=0, tiled=True),
    )


def norm_rows(own_part):
    return lax.all_gather(own_part, "tensor", axis=0, tiled=True)


def grad_rows(own_part):
    return lax.all_gather(own_part, "tensor", axis=0, tiled=True)


def branch_sum(mixture, weight):
    return lax.psum_scatter(
        jnp.dot(mixture, weight, preferred_element_type=jnp.float32),
        "tensor",
        scatter_dimension=0,
        tiled=True,
    )


def input_grad(grad_term, own_rows):
    return lax.psum_scatter(
        grad_term(jnp.int32(0), own_rows * lax.axis_size("tensor")),
        "tensor",
        scatter_dimension=0,
        tiled=True,
    )


def head_view(matrix):
    return matrix.reshape(matrix.shape[0], -1, DH)


def block_scores(query_block, key_heads, first_row, causal, length):
    scores = jnp.einsum("qhd,khd->hqk", query_block, key_heads, preferred_element_type=jnp.float32)
    scores = scores * DH ** (-0.5)
    row_ids = first_row + jnp.arange(query_block.shape[0])
    col_ids = jnp.arange(key_heads.shape[0])
    live_mask = col_ids[None, :] < length
    if causal:
        live_mask = live_mask & (col_ids[None, :] <= row_ids[:, None])
    return jnp.where(live_mask[None], scores, MASKED)


def attend_forward(queries, key_rows, value_rows, causal, length):
    row_total = queries.shape[0]
    block_size = min(BLOCK_ROWS, row_total)
    blocks = row_total // block_size
    query_heads = head_view(queries).reshape(blocks, block_size, -1, DH)
    key_heads = head_view(key_rows)
    value_heads = head_view(value_rows)

    def one_block(members):
        query_block, block_index = members
        scores = block_scores(query_block, key_heads, block_index * block_size, causal, length)
        row_max = jnp.max(scores, axis=-1, keepdims=True)
        shifted = jnp.exp(scores - row_max)
        summed = jnp.sum(shifted, axis=-1, keepdims=True)
        weights = (shifted / summed).astype(jnp.bfloat16)
        mixture = jnp.einsum(
            "hqk,khd->qhd", weights, value_heads, preferred_element_type=jnp.float32
        )
        return (mixture.astype(jnp.bfloat16), (row_max + jnp.log(summed))[..., 0])

    mixture, log_norm = lax.map(one_block, (query_heads, jnp.arange(blocks)))
    return (mixture.reshape(row_total, -1), log_norm)


def attend_backward(queries, key_rows, value_rows, grad_mix, log_norm, causal, length):
    row_total = queries.shape[0]
    block_size = min(BLOCK_ROWS, row_total)
    blocks = row_total // block_size
    query_heads = head_view(queries).reshape(blocks, block_size, -1, DH)
    grad_heads = head_view(grad_mix).reshape(blocks, block_size, -1, DH)
    key_heads = head_view(key_rows)
    value_heads = head_view(value_rows)
    scale_value = DH ** (-0.5)

    def one_block(carry, members):
        query_block, grad_block, norm_block, block_index = members
        scores = block_scores(query_block, key_heads, block_index * block_size, causal, length)
        probs = jnp.exp(scores - norm_block[..., None])
        grad_probs = jnp.einsum(
            "qhd,khd->hqk", grad_block, value_heads, preferred_element_type=jnp.float32
        )
        inner = jnp.sum(probs * grad_probs, axis=-1, keepdims=True)
        grad_scores = (probs * (grad_probs - inner)).astype(jnp.bfloat16)
        grad_query = (
            jnp.einsum("hqk,khd->qhd", grad_scores, key_heads, preferred_element_type=jnp.float32)
            * scale_value
        )
        key_sum, value_sum = carry
        key_sum = (
            key_sum
            + jnp.einsum(
                "hqk,qhd->khd", grad_scores, query_block, preferred_element_type=jnp.float32
            )
            * scale_value
        )
        value_sum = value_sum + jnp.einsum(
            "hqk,qhd->khd",
            probs.astype(jnp.bfloat16),
            grad_block,
            preferred_element_type=jnp.float32,
        )
        return ((key_sum, value_sum), grad_query)

    zeros = jnp.zeros(key_heads.shape, jnp.float32)
    (key_sum, value_sum), grad_query = lax.scan(
        one_block, (zeros, zeros), (query_heads, grad_heads, log_norm, jnp.arange(blocks))
    )
    key_total = key_rows.shape[0]
    return (
        grad_query.reshape(row_total, -1),
        key_sum.reshape(key_total, -1),
        value_sum.reshape(key_total, -1),
    )


def widened(shard, dim, factor):
    shape_list = list(shard.shape)
    shape_list[dim] = shape_list[dim] * factor
    return jnp.zeros(shape_list, jnp.float32)


def body(
    inputs,
    memory,
    tgt_len,
    src_len,
    cotangent,
    w_qkv,
    w_out,
    cross_query,
    cross_kv,
    cross_out,
    ffn_up,
    ffn_down,
    gain_one,
    bias_one,
    gain_two,
    bias_two,
    gain_three,
    bias_three,
):
    own_rows = inputs.shape[1]
    row_first = lax.axis_index("tensor") * own_rows
    shards = (
        w_qkv,
        w_out,
        cross_query,
        cross_kv,
        cross_out,
        ffn_up,
        ffn_down,
        gain_one,
        bias_one,
        gain_two,
        bias_two,
        gain_three,
        bias_three,
    )
    shard_dims = (1, 1, 0, 1, 1, 0, 1, 0, 0, 0, 0, 0, 0)
    dp_count = lax.axis_size("dp")
    accum_list = [
        widened(shard, dim_index, dp_count) for shard, dim_index in zip(shards, shard_dims)
    ]
    accum_init = tuple(accum_list)

    def advance(accum, members):
        own_in, own_memory, tgt_count, src_count, own_cot = members
        gathered = gather_weights(*shards)
        live_rows = (row_first + jnp.arange(own_rows) < tgt_count).astype(jnp.float32)[:, None]
        residual_in = own_in.astype(jnp.float32)
        normed, pull_one = jax.vjp(
            layer_norm,
            residual_in,
            gathered[7].astype(jnp.float32),
            gathered[8].astype(jnp.float32),
        )
        normed_all = norm_rows(normed.astype(jnp.bfloat16))
        projected = jnp.einsum(
            "td,jdh->jth", normed_all, gathered[0], preferred_element_type=jnp.float32
        ).astype(jnp.bfloat16)
        self_mix, self_norm = attend_forward(
            projected[0], projected[1], projected[2], True, tgt_count
        )
        hidden_one = residual_in + branch_sum(self_mix, gathered[1])
        normed, pull_two = jax.vjp(
            layer_norm,
            hidden_one,
            gathered[9].astype(jnp.float32),
            gathered[10].astype(jnp.float32),
        )
        cross_all, memory_all = (
            lax.all_gather(normed.astype(jnp.bfloat16), "tensor", axis=0, tiled=True),
            lax.all_gather(own_memory, "tensor", axis=0, tiled=True),
        )
        cross_queries = jnp.dot(cross_all, gathered[2], preferred_element_type=jnp.float32).astype(
            jnp.bfloat16
        )
        cross_pair = jnp.einsum(
            "sd,jdh->jsh", memory_all, gathered[3], preferred_element_type=jnp.float32
        ).astype(jnp.bfloat16)
        cross_mix, cross_norm = attend_forward(
            cross_queries, cross_pair[0], cross_pair[1], False, src_count
        )
        hidden_two = hidden_one + branch_sum(cross_mix, gathered[4])
        normed, pull_three = jax.vjp(
            layer_norm,
            hidden_two,
            gathered[11].astype(jnp.float32),
            gathered[12].astype(jnp.float32),
        )
        grad_out = live_rows * own_cot.astype(jnp.float32)
        ffn_rows = norm_rows(normed.astype(jnp.bfloat16))
        before = jnp.dot(ffn_rows, gathered[5], preferred_element_type=jnp.float32)
        gated, gate_pull = jax.vjp(smooth_gate, before)
        active = gated.astype(jnp.bfloat16)
        output = live_rows * (hidden_two + branch_sum(active, gathered[6]))
        grad_all = grad_rows(grad_out.astype(jnp.bfloat16))
        grad_down = jnp.einsum("tf,td->fd", active, grad_all, preferred_element_type=jnp.float32)
        grad_active = jnp.einsum(
            "td,fd->tf", grad_all, gathered[6], preferred_element_type=jnp.float32
        )
        grad_before = gate_pull(grad_active)[0].astype(jnp.bfloat16)
        grad_up = jnp.einsum("td,tf->df", ffn_rows, grad_before, preferred_element_type=jnp.float32)

        def ffn_term(first_row, row_count):
            return jnp.einsum(
                "tf,df->td", grad_before, gathered[5], preferred_element_type=jnp.float32
            )

        back_three = input_grad(ffn_term, own_rows)
        grad_hidden, grad_gain_three, grad_bias_three = pull_three(back_three)
        grad_two = grad_out + grad_hidden
        grad_all = grad_rows(grad_two.astype(jnp.bfloat16))
        grad_cross = jnp.einsum(
            "th,td->hd", cross_mix, grad_all, preferred_element_type=jnp.float32
        )
        grad_mix = jnp.einsum(
            "td,hd->th", grad_all, gathered[4], preferred_element_type=jnp.float32
        ).astype(jnp.bfloat16)
        grad_cq, grad_ck, grad_cv = attend_backward(
            cross_queries, cross_pair[0], cross_pair[1], grad_mix, cross_norm, False, src_count
        )
        grad_cq = grad_cq.astype(jnp.bfloat16)
        grad_ckv = jnp.stack([grad_ck, grad_cv]).astype(jnp.bfloat16)
        grad_query = jnp.einsum("td,th->dh", cross_all, grad_cq, preferred_element_type=jnp.float32)
        grad_pair = jnp.einsum(
            "sd,jsh->jdh", memory_all, grad_ckv, preferred_element_type=jnp.float32
        )
        back_rows = jnp.einsum(
            "th,dh->td", grad_cq, gathered[2], preferred_element_type=jnp.float32
        )
        back_memory = jnp.einsum(
            "jsh,jdh->sd", grad_ckv, gathered[3], preferred_element_type=jnp.float32
        )
        own_back, grad_encoded = (
            lax.psum_scatter(back_rows, "tensor", scatter_dimension=0, tiled=True),
            lax.psum_scatter(back_memory, "tensor", scatter_dimension=0, tiled=True),
        )
        grad_hidden, grad_gain_two, grad_bias_two = pull_two(own_back)
        grad_one = grad_two + grad_hidden
        grad_all = grad_rows(grad_one.astype(jnp.bfloat16))
        grad_self_out = jnp.einsum(
            "th,td->hd", self_mix, grad_all, preferred_element_type=jnp.float32
        )
        grad_mix = jnp.einsum(
            "td,hd->th", grad_all, gathered[1], preferred_element_type=jnp.float32
        ).astype(jnp.bfloat16)
        grad_sq, grad_sk, grad_sv = attend_backward(
            projected[0], projected[1], projected[2], grad_mix, self_norm, True, tgt_count
        )
        grad_triple = jnp.stack([grad_sq, grad_sk, grad_sv]).astype(jnp.bfloat16)
        grad_qkv = jnp.einsum(
            "td,jth->jdh", normed_all, grad_triple, preferred_element_type=jnp.float32
        )

        def self_term(first_row, row_count):
            return jnp.einsum(
                "jth,jdh->td", grad_triple, gathered[0], preferred_element_type=jnp.float32
            )

        grad_hidden, grad_gain_one, grad_bias_one = pull_one(input_grad(self_term, own_rows))
        grad_values = grad_one + grad_hidden
        grads = (
            grad_qkv,
            grad_self_out,
            grad_query,
            grad_pair,
            grad_cross,
            grad_up,
            grad_down,
            grad_gain_one,
            grad_bias_one,
            grad_gain_two,
            grad_bias_two,
            grad_gain_three,
            grad_bias_three,
        )
        accum = jax.tree.map(jnp.add, accum, grads)
        return (accum, (output.astype(jnp.bfloat16), grad_values, grad_encoded))

    accum, (outputs, grad_inputs, grad_memory) = lax.scan(
        advance, accum_init, (inputs, memory, tgt_len, src_len, cotangent)
    )
    accum_list = list(accum)
    accum = reduce_grads(*accum_list)
    norm_grads = lax.psum((accum[7], accum[8], accum[9], accum[10], accum[11], accum[12]), "tensor")
    return (
        outputs,
        grad_inputs,
        grad_memory,
        accum[0],
        accum[1],
        accum[2],
        accum[3],
        accum[4],
        accum[5],
        accum[6],
        norm_grads[0],
        norm_grads[1],
        norm_grads[2],
        norm_grads[3],
        norm_grads[4],
        norm_grads[5],
    )


def solution(mesh):
    return jax.shard_map(
        body,
        mesh=mesh,
        in_specs=(
            P("dp", "tensor", None),
            P("dp", "tensor", None),
            P("dp"),
            P("dp"),
            P("dp", "tensor", None),
            P(None, "dp", "tensor"),
            P("tensor", "dp"),
            P("dp", "tensor"),
            P(None, "dp", "tensor"),
            P("tensor", "dp"),
            P("dp", "tensor"),
            P("tensor", "dp"),
            P("dp"),
            P("dp"),
            P("dp"),
            P("dp"),
            P("dp"),
            P("dp"),
        ),
        out_specs=(
            P("dp", "tensor", None),
            P("dp", "tensor", None),
            P("dp", "tensor", None),
            P(None, "dp", "tensor"),
            P("tensor", "dp"),
            P("dp", "tensor"),
            P(None, "dp", "tensor"),
            P("tensor", "dp"),
            P("dp", "tensor"),
            P("tensor", "dp"),
            P("dp"),
            P("dp"),
            P("dp"),
            P("dp"),
            P("dp"),
            P("dp"),
        ),
        check_vma=False,
    )
```

profile of v0, /device:TPU:0, one launch (start us, length us, event | category | flops | bytes accessed | tf_op | source)
XLA Modules:
  0.0 1706.3 jit_solution(2830867907719155688)
XLA Ops:
  8.2 1231.4 %while.159 = (s32[]{:T(128)}, f32[3,512,128]{1,2,0:T(8,128)}, f32[128,512]{1,0:T(8,128)}, f32[512,128]{1,0:T(8,128)}, f32[2,512,128]{1,2,0:T(8,128)}, /*index=5*...) while((s32[]{:T(128)}, f32[3,512,128]{1,2,0:T(8,128)}, ...), condition=%wide.region_40.41_spmd.clone, body=%wide.region_0.40_spmd.clone.sunk | while | flops 8421522944 | bytes 381262368 | solution.py:387
  41.5 23.9 %all-reduce.22 = (bf16[512]{0:T(512)(128)(2,1)S(1)}, bf16[512]{0:T(512)(128)(2,1)S(1)}, bf16[512]{0:T(512)(128)(2,1)S(1)}, bf16[512]{0:T(512)(128)(2,1)S(1)}, bf...) all-reduce(bf16[512]{0:T(512)(128)(2,1)S(1)} %dynamic-update-slice.18, ...), channel_id=1, replica_groups=mesh['dp'=8,'tensor'=4] {'dp'}, use_global_device_ids=true, to_apply=%add.1 | all-reduce | flops 3072 | bytes 12288 | tf_op jit(solution)/shard_map/while
  68.6 30.7 %all_gather.148 = bf16[128,512]{0,1:T(8,128)(2,1)S(1)} all-gather(bf16[128,64]{0,1:T(8,128)(2,1)} %get-tuple-element.2082), channel_id=1, replica_groups=mesh['dp'=8,'tensor'=4] {'dp'}, dimensions={1}, use_global_device_ids=true | all-gather | bytes 147456 | tf_op jit(solution)/shard_map/while/body/eval_jaxpr/all_gather | solution.py:39
  99.3 31.2 %all_gather.147 = bf16[3,512,128]{2,1,0:T(8,128)(2,1)S(1)} all-gather(bf16[3,64,128]{2,1,0:T(8,128)(2,1)} %get-tuple-element.2077), channel_id=1, replica_groups=mesh['dp'=8,'tensor'=4] {'dp'}, dimensions={1}, use_global_device_ids=true | all-gather | bytes 442368 | tf_op jit(solution)/shard_map/while/body/eval_jaxpr/all_gather | solution.py:38
  133.4 12.2 while.160
  149.5 27.9 %reduce-scatter.29.cloned.1.call-done = f32[256,512]{1,0:T(8,128)} async-done(((f32[1024,512]{1,0:T(8,128)}), f32[256,512]{1,0:T(8,128)}) %reduce-scatter.29.cloned.1.call-update) | async-done | bytes 524304 | tf_op jit(solution)/shard_map/while/body/eval_jaxpr/reduce_scatter | solution.py:95
  180.4 30.6 %all_gather.154 = bf16[128,512]{0,1:T(8,128)(2,1)S(1)} all-gather(bf16[128,64]{0,1:T(8,128)(2,1)S(1)} %copy-done.65), channel_id=1, replica_groups=mesh['dp'=8,'tensor'=4] {'dp'}, dimensions={1}, use_global_device_ids=true | all-gather | bytes 147456 | tf_op jit(solution)/shard_map/while/body/eval_jaxpr/all_gather | solution.py:42
  210.9 30.5 %all_gather.150 = bf16[512,128]{1,0:T(8,128)(2,1)S(1)} all-gather(bf16[64,128]{1,0:T(8,128)(2,1)S(1)} %copy-done.64), channel_id=1, replica_groups=mesh['dp'=8,'tensor'=4] {'dp'}, dimensions={0}, use_global_device_ids=true | all-gather | bytes 147456 | tf_op jit(solution)/shard_map/while/body/eval_jaxpr/all_gather | solution.py:40
  241.4 30.7 %all_gather.151 = bf16[2,512,128]{2,1,0:T(8,128)(2,1)S(1)} all-gather(bf16[2,64,128]{2,1,0:T(8,128)(2,1)S(1)} %copy-done.50), channel_id=1, replica_groups=mesh['dp'=8,'tensor'=4] {'dp'}, dimensions={1}, use_global_device_ids=true | all-gather | bytes 294912 | tf_op jit(solution)/shard_map/while/body/eval_jaxpr/all_gather | solution.py:41
  276.5 8.1 while.161
  290.4 28.5 %reduce-scatter.31.cloned.1.call-done = f32[256,512]{1,0:T(8,128)} async-done(((f32[1024,512]{1,0:T(8,128)}), f32[256,512]{1,0:T(8,128)}) %reduce-scatter.31.cloned.1.call-update) | async-done | bytes 524304 | tf_op jit(solution)/shard_map/while/body/eval_jaxpr/reduce_scatter | solution.py:95
  321.3 33.6 %all_gather.156 = bf16[512,512]{1,0:T(8,128)(2,1)} all-gather(bf16[64,512]{1,0:T(8,128)(2,1)S(1)} %copy-done.38), channel_id=1, replica_groups=mesh['dp'=8,'tensor'=4] {'dp'}, dimensions={0}, use_global_device_ids=true | all-gather | bytes 589824 | tf_op jit(solution)/shard_map/while/body/eval_jaxpr/all_gather | solution.py:43
  355.0 31.2 %all_gather.153 = bf16[512,512]{0,1:T(8,128)(2,1)S(1)} all-gather(bf16[512,64]{0,1:T(8,128)(2,1)S(1)} %copy-done.37), channel_id=1, replica_groups=mesh['dp'=8,'tensor'=4] {'dp'}, dimensions={1}, use_global_device_ids=true | all-gather | bytes 589824 | tf_op jit(solution)/shard_map/while/body/eval_jaxpr/all_gather | solution.py:44
  386.2 3.5 fusion.336
  389.7 5.3 fusion.340
  398.1 31.7 %reduce-scatter.33.cloned.1.call-done = f32[256,512]{1,0:T(8,128)} async-done(((f32[1024,512]{1,0:T(8,128)}), f32[256,512]{1,0:T(8,128)}) %reduce-scatter.33.cloned.1.call-update) | async-done | bytes 524304 | tf_op jit(solution)/shard_map/while/body/eval_jaxpr/reduce_scatter | solution.py:104
  434.7 16.8 all-gather.22.cloned.1.call-done
  457.9 13.5 while.162
  472.8 2.8 fusion.344
  475.6 31.5 %reduce-scatter.35.cloned.1.call-done = f32[256,512]{1,0:T(8,128)} async-done(((f32[1024,512]{1,0:T(8,128)}), f32[256,512]{1,0:T(8,128)}) %reduce-scatter.35.cloned.1.call-update) | async-done | bytes 524304 | tf_op jit(solution)/shard_map/while/body/eval_jaxpr/reduce_scatter | solution.py:342
  512.5 3.9 fusion.351
  520.3 9.0 all-gather.24.cloned.1.call-done
  532.4 21.7 %while.163 = (s32[]{:T(128)}, f32[1024,2,64]{0,2,1:T(8,128)S(1)}, f32[1024,2,64]{0,2,1:T(8,128)}, bf16[2,512,2,64]{1,3,2,0:T(8,128)(2,1)}, bf16[2,512,2,64]{1,3,...) while((s32[]{:T(128)}, f32[1024,2,64]{0,2,1:T(8,128)S(1)}, ...), condition=%wide.region_28.28_spmd.clone, body=%wide.region_26.27_spmd.clone.sunk | while | flops 688587264 | bytes 37259468 | solution.py:191
  545.8 3.2 fusion.389
  559.8 3.1 convolution_add_fusion.13
  573.1 24.2 %reduce-scatter.41.cloned.1.call-done = f32[256,512]{1,0:T(8,128)} async-done(((f32[1024,512]{1,0:T(8,128)}), f32[256,512]{1,0:T(8,128)}) %reduce-scatter.41.cloned.1.call-update) | async-done | bytes 524304 | tf_op jit(solution)/shard_map/while/body/eval_jaxpr/reduce_scatter | solution.py:343
  601.6 2.9 fusion.347
  604.5 26.7 %reduce-scatter.37.cloned.1.call-done = f32[256,512]{1,0:T(8,128)} async-done(((f32[1024,512]{1,0:T(8,128)}), f32[256,512]{1,0:T(8,128)}) %reduce-scatter.37.cloned.1.call-update) | async-done | bytes 524304 | tf_op jit(solution)/shard_map/while/body/eval_jaxpr/reduce_scatter | solution.py:104
  645.6 22.1 %all-reduce.22 = (bf16[512]{0:T(512)(128)(2,1)S(1)}, bf16[512]{0:T(512)(128)(2,1)S(1)}, bf16[512]{0:T(512)(128)(2,1)S(1)}, bf16[512]{0:T(512)(128)(2,1)S(1)}, bf...) all-reduce(bf16[512]{0:T(512)(128)(2,1)S(1)} %dynamic-update-slice.18, ...), channel_id=1, replica_groups=mesh['dp'=8,'tensor'=4] {'dp'}, use_global_device_ids=true, to_apply=%add.1 | all-reduce | flops 3072 | bytes 12288 | tf_op jit(solution)/shard_map/while
  670.9 30.7 %all_gather.148 = bf16[128,512]{0,1:T(8,128)(2,1)S(1)} all-gather(bf16[128,64]{0,1:T(8,128)(2,1)} %get-tuple-element.2082), channel_id=1, replica_groups=mesh['dp'=8,'tensor'=4] {'dp'}, dimensions={1}, use_global_device_ids=true | all-gather | bytes 147456 | tf_op jit(solution)/shard_map/while/body/eval_jaxpr/all_gather | solution.py:39
  701.6 31.2 %all_gather.147 = bf16[3,512,128]{2,1,0:T(8,128)(2,1)S(1)} all-gather(bf16[3,64,128]{2,1,0:T(8,128)(2,1)} %get-tuple-element.2077), channel_id=1, replica_groups=mesh['dp'=8,'tensor'=4] {'dp'}, dimensions={1}, use_global_device_ids=true | all-gather | bytes 442368 | tf_op jit(solution)/shard_map/while/body/eval_jaxpr/all_gather | solution.py:38
  735.7 12.2 while.160
  751.7 27.0 %reduce-scatter.29.cloned.1.call-done = f32[256,512]{1,0:T(8,128)} async-done(((f32[1024,512]{1,0:T(8,128)}), f32[256,512]{1,0:T(8,128)}) %reduce-scatter.29.cloned.1.call-update) | async-done | bytes 524304 | tf_op jit(solution)/shard_map/while/body/eval_jaxpr/reduce_scatter | solution.py:95
  781.7 30.6 %all_gather.154 = bf16[128,512]{0,1:T(8,128)(2,1)S(1)} all-gather(bf16[128,64]{0,1:T(8,128)(2,1)S(1)} %copy-done.65), channel_id=1, replica_groups=mesh['dp'=8,'tensor'=4] {'dp'}, dimensions={1}, use_global_device_ids=true | all-gather | bytes 147456 | tf_op jit(solution)/shard_map/while/body/eval_jaxpr/all_gather | solution.py:42
  812.3 30.5 %all_gather.150 = bf16[512,128]{1,0:T(8,128)(2,1)S(1)} all-gather(bf16[64,128]{1,0:T(8,128)(2,1)S(1)} %copy-done.64), channel_id=1, replica_groups=mesh['dp'=8,'tensor'=4] {'dp'}, dimensions={0}, use_global_device_ids=true | all-gather | bytes 147456 | tf_op jit(solution)/shard_map/while/body/eval_jaxpr/all_gather | solution.py:40
  842.8 30.7 %all_gather.151 = bf16[2,512,128]{2,1,0:T(8,128)(2,1)S(1)} all-gather(bf16[2,64,128]{2,1,0:T(8,128)(2,1)S(1)} %copy-done.50), channel_id=1, replica_groups=mesh['dp'=8,'tensor'=4] {'dp'}, dimensions={1}, use_global_device_ids=true | all-gather | bytes 294912 | tf_op jit(solution)/shard_map/while/body/eval_jaxpr/all_gather | solution.py:41
  877.8 8.1 while.161
  891.8 28.5 %reduce-scatter.31.cloned.1.call-done = f32[256,512]{1,0:T(8,128)} async-done(((f32[1024,512]{1,0:T(8,128)}), f32[256,512]{1,0:T(8,128)}) %reduce-scatter.31.cloned.1.call-update) | async-done | bytes 524304 | tf_op jit(solution)/shard_map/while/body/eval_jaxpr/reduce_scatter | solution.py:95
  922.7 33.6 %all_gather.156 = bf16[512,512]{1,0:T(8,128)(2,1)} all-gather(bf16[64,512]{1,0:T(8,128)(2,1)S(1)} %copy-done.38), channel_id=1, replica_groups=mesh['dp'=8,'tensor'=4] {'dp'}, dimensions={0}, use_global_device_ids=true | all-gather | bytes 589824 | tf_op jit(solution)/shard_map/while/body/eval_jaxpr/all_gather | solution.py:43
  956.3 31.2 %all_gather.153 = bf16[512,512]{0,1:T(8,128)(2,1)S(1)} all-gather(bf16[512,64]{0,1:T(8,128)(2,1)S(1)} %copy-done.37), channel_id=1, replica_groups=mesh['dp'=8,'tensor'=4] {'dp'}, dimensions={1}, use_global_device_ids=true | all-gather | bytes 589824 | tf_op jit(solution)/shard_map/while/body/eval_jaxpr/all_gather | solution.py:44
  987.5 3.5 fusion.336
  991.0 5.3 fusion.340
  999.4 31.6 %reduce-scatter.33.cloned.1.call-done = f32[256,512]{1,0:T(8,128)} async-done(((f32[1024,512]{1,0:T(8,128)}), f32[256,512]{1,0:T(8,128)}) %reduce-scatter.33.cloned.1.call-update) | async-done | bytes 524304 | tf_op jit(solution)/shard_map/while/body/eval_jaxpr/reduce_scatter | solution.py:104
  1036.0 16.8 all-gather.22.cloned.1.call-done
  1059.2 13.5 while.162
  1074.0 2.8 fusion.344
  1076.9 31.5 %reduce-scatter.35.cloned.1.call-done = f32[256,512]{1,0:T(8,128)} async-done(((f32[1024,512]{1,0:T(8,128)}), f32[256,512]{1,0:T(8,128)}) %reduce-scatter.35.cloned.1.call-update) | async-done | bytes 524304 | tf_op jit(solution)/shard_map/while/body/eval_jaxpr/reduce_scatter | solution.py:342
  1113.8 3.9 fusion.351
  1121.6 9.0 all-gather.24.cloned.1.call-done
  1133.7 21.7 %while.163 = (s32[]{:T(128)}, f32[1024,2,64]{0,2,1:T(8,128)S(1)}, f32[1024,2,64]{0,2,1:T(8,128)}, bf16[2,512,2,64]{1,3,2,0:T(8,128)(2,1)}, bf16[2,512,2,64]{1,3,...) while((s32[]{:T(128)}, f32[1024,2,64]{0,2,1:T(8,128)S(1)}, ...), condition=%wide.region_28.28_spmd.clone, body=%wide.region_26.27_spmd.clone.sunk | while | flops 688587264 | bytes 37259468 | solution.py:191
  1147.1 3.2 fusion.389
  1161.1 3.5 convolution_add_fusion.13
  1175.7 22.8 %reduce-scatter.41.cloned.1.call-done = f32[256,512]{1,0:T(8,128)} async-done(((f32[1024,512]{1,0:T(8,128)}), f32[256,512]{1,0:T(8,128)}) %reduce-scatter.41.cloned.1.call-update) | async-done | bytes 524304 | tf_op jit(solution)/shard_map/while/body/eval_jaxpr/reduce_scatter | solution.py:343
  1202.8 3.1 fusion.347
  1205.9 26.6 %reduce-scatter.37.cloned.1.call-done = f32[256,512]{1,0:T(8,128)} async-done(((f32[1024,512]{1,0:T(8,128)}), f32[256,512]{1,0:T(8,128)}) %reduce-scatter.37.cloned.1.call-update) | async-done | bytes 524304 | tf_op jit(solution)/shard_map/while/body/eval_jaxpr/reduce_scatter | solution.py:104
  1251.9 37.1 %all-reduce.19 = (f32[512]{0:T(512)S(1)}, f32[512]{0:T(512)S(1)}, f32[512]{0:T(512)S(1)}, f32[512]{0:T(512)S(1)}, f32[512]{0:T(512)S(1)}, /*index=5*/f32[512]{0:T(512)S(1)}) all-reduce(f32[512]{0:T(512)S(1)} %copy-done.95, f32[512]{0:T(512)S(1)} %copy-done.92, ...), channel_id=17, replica_groups=mesh['dp'=8,'tensor'=4] {'dp'}, use_global_device_ids=true, to_apply=%region_48.49.clone | all-reduce | flops 3072 | bytes 24576
  1289.4 6.4 all-reduce.20
  1295.9 9.5 reduce-scatter.19.cloned.1.call-done
  1305.4 64.1 %reduce-scatter.17.cloned.1.call-done = f32[128,64]{0,1:T(8,128)} async-done(((f32[128,512]{0,1:T(8,128)}), f32[128,64]{0,1:T(8,128)}) %reduce-scatter.17.cloned.1.call-update) | async-done | bytes 32784 | tf_op jit(solution)/shard_map/reduce_scatter | solution.py:71
  1369.5 64.2 %reduce-scatter.23.cloned.1.call-done = f32[128,64]{0,1:T(8,128)} async-done(((f32[128,512]{0,1:T(8,128)}), f32[128,64]{0,1:T(8,128)}) %reduce-scatter.23.cloned.1.call-update) | async-done | bytes 32784 | tf_op jit(solution)/shard_map/reduce_scatter | solution.py:74
  1433.7 65.0 %reduce-scatter.21.cloned.1.call-done = f32[2,64,128]{2,1,0:T(8,128)} async-done(((f32[2,512,128]{2,1,0:T(8,128)}), f32[2,64,128]{2,1,0:T(8,128)}) %reduce-scatter.21.cloned.1.call-update) | async-done | bytes 65552 | tf_op jit(solution)/shard_map/reduce_scatter | solution.py:73
  1498.7 66.6 %reduce-scatter.15.cloned.1.call-done = f32[3,64,128]{2,1,0:T(8,128)} async-done(((f32[3,512,128]{2,1,0:T(8,128)}), f32[3,64,128]{2,1,0:T(8,128)}) %reduce-scatter.15.cloned.1.call-update) | async-done | bytes 98320 | tf_op jit(solution)/shard_map/reduce_scatter | solution.py:70
  1565.3 66.6 %reduce-scatter.25.cloned.1.call-done = f32[64,512]{1,0:T(8,128)} async-done(((f32[512,512]{1,0:T(8,128)}), f32[64,512]{1,0:T(8,128)}) %reduce-scatter.25.cloned.1.call-update) | async-done | bytes 131088 | tf_op jit(solution)/shard_map/reduce_scatter | solution.py:75
  1631.9 66.8 %reduce-scatter.27.cloned.1.call-done = f32[512,64]{0,1:T(8,128)} async-done(((f32[512,512]{0,1:T(8,128)}), f32[512,64]{0,1:T(8,128)}) %reduce-scatter.27.cloned.1.call-update) | async-done | bytes 131088 | tf_op jit(solution)/shard_map/reduce_scatter | solution.py:76
  (856 shorter events, 283.5 us)
Async XLA Ops:
  32.2 98.4 %all-gather.12.cloned.1.call-start = ((), (), s32[]{:S(2)}) async-start(), calls=%async_computation.21 | async-start | bytes 1310720 | tf_op jit(solution)/shard_map/while/body/eval_jaxpr/all_gather | solution.py:87
  33.3 66.0 %copy-start.44 = (f32[256]{0:T(256)}, f32[256]{0:T(256)S(1)}, u32[]{:S(2)}) copy-start(f32[256]{0:T(256)S(1)} %broadcast_multiply_fusion.6) | copy-start | bytes 3076 | tf_op jit(solution)/shard_map/while
  34.5 64.8 %copy-start.58 = (f32[256]{0:T(256)}, f32[256]{0:T(256)S(1)}, u32[]{:S(2)}) copy-start(f32[256]{0:T(256)S(1)} %fusion.326) | copy-start | bytes 3076 | tf_op jit(solution)/shard_map/while
  67.3 110.1 %reduce-scatter.29.cloned.1.call-start = ((), (), s32[]{:S(2)}) async-start(), calls=%async_computation.22 | async-start | bytes 2621440 | tf_op jit(solution)/shard_map/while/body/eval_jaxpr/reduce_scatter | solution.py:95
  146.8 64.2 %copy-start.64 = (bf16[64,128]{1,0:T(8,128)(2,1)S(1)}, bf16[64,128]{1,0:T(8,128)(2,1)}, u32[]{:S(2)}) copy-start(bf16[64,128]{1,0:T(8,128)(2,1)} %get-tuple-element.2085) | copy-start | bytes 49156 | tf_op jit(solution)/shard_map/while
  146.8 94.7 %copy-start.50 = (bf16[2,64,128]{2,1,0:T(8,128)(2,1)S(1)}, bf16[2,64,128]{2,1,0:T(8,128)(2,1)}, u32[]{:S(2)}) copy-start(bf16[2,64,128]{2,1,0:T(8,128)(2,1)} %get-tuple-element.2087) | copy-start | bytes 98308 | tf_op jit(solution)/shard_map/while
  148.6 123.6 %all-gather.16.cloned.1.call-start = ((), (), s32[]{:S(2)}) async-start(), calls=%async_computation.24 | async-start | bytes 1310720 | tf_op jit(solution)/shard_map/while/body/eval_jaxpr/all_gather | solution.py:279
  149.4 124.7 %all-gather.14.cloned.1.call-start = ((), (), s32[]{:S(2)}) async-start(), calls=%async_computation.23 | async-start | bytes 1310720 | tf_op jit(solution)/shard_map/while/body/eval_jaxpr/all_gather | solution.py:278
  149.5 126.5 %copy-start.46 = (f32[512]{0:T(512)}, f32[512]{0:T(512)S(1)}, u32[]{:S(2)}) copy-start(f32[512]{0:T(512)S(1)} %convert_element_type.395) | copy-start | bytes 6148 | tf_op jit(solution)/shard_map/while
  178.6 97.8 %copy-start.54 = (f32[256]{0:T(256)}, f32[256]{0:T(256)S(1)}, u32[]{:S(2)}) copy-start(f32[256]{0:T(256)S(1)} %broadcast_multiply_fusion.7) | copy-start | bytes 3076 | tf_op jit(solution)/shard_map/while
  178.8 97.6 %copy-start.70 = (f32[256]{0:T(256)}, f32[256]{0:T(256)S(1)}, u32[]{:S(2)}) copy-start(f32[256]{0:T(256)S(1)} %multiply_reduce_fusion.14) | copy-start | bytes 3076 | tf_op jit(solution)/shard_map/while
  178.8 97.6 %copy-start.60 = (f32[256]{0:T(256)}, f32[256]{0:T(256)S(1)}, u32[]{:S(2)}) copy-start(f32[256]{0:T(256)S(1)} %fusion.332) | copy-start | bytes 3076 | tf_op jit(solution)/shard_map/while
  179.7 139.2 %reduce-scatter.31.cloned.1.call-start = ((), (), s32[]{:S(2)}) async-start(), calls=%async_computation.26 | async-start | bytes 2621440 | tf_op jit(solution)/shard_map/while/body/eval_jaxpr/reduce_scatter | solution.py:95
  285.6 69.4 %copy-start.37 = (bf16[512,64]{0,1:T(8,128)(2,1)S(1)}, bf16[512,64]{0,1:T(8,128)(2,1)}, u32[]{:S(2)}) copy-start(bf16[512,64]{0,1:T(8,128)(2,1)} %get-tuple-element.2081) | copy-start | bytes 196612 | tf_op jit(solution)/shard_map/while
  287.4 98.8 %all-gather.18.cloned.1.call-start = ((), (), s32[]{:S(2)}) async-start(), calls=%async_computation.25 | async-start | bytes 1310720 | tf_op jit(solution)/shard_map/while/body/eval_jaxpr/all_gather | solution.py:91
  289.0 100.7 %all-gather.20.cloned.1.call-start = ((), (), s32[]{:S(2)}) async-start(), calls=%async_computation.27 | async-start | bytes 1310720 | tf_op jit(solution)/shard_map/while/body/eval_jaxpr/all_gather | solution.py:87
  289.7 65.2 %copy-start.48 = (f32[512]{0:T(512)}, f32[512]{0:T(512)S(1)}, u32[]{:S(2)}) copy-start(f32[512]{0:T(512)S(1)} %convert_element_type.397) | copy-start | bytes 6148 | tf_op jit(solution)/shard_map/while
  321.3 108.5 %reduce-scatter.33.cloned.1.call-start = ((), (), s32[]{:S(2)}) async-start(), calls=%async_computation.28 | async-start | bytes 2621440 | tf_op jit(solution)/shard_map/while/body/eval_jaxpr/reduce_scatter | solution.py:104
  398.0 53.5 %all-gather.22.cloned.1.call-start = ((), (), s32[]{:S(2)}) async-start(), calls=%async_computation.29 | async-start | bytes 1310720 | tf_op jit(solution)/shard_map/while/body/eval_jaxpr/all_gather | solution.py:91
  434.6 72.5 %reduce-scatter.35.cloned.1.call-start = ((), (), s32[]{:S(2)}) async-start(), calls=%async_computation.30 | async-start | bytes 2621440 | tf_op jit(solution)/shard_map/while/body/eval_jaxpr/reduce_scatter | solution.py:342
  475.6 53.8 %all-gather.24.cloned.1.call-start = ((), (), s32[]{:S(2)}) async-start(), calls=%async_computation.31 | async-start | bytes 1310720 | tf_op jit(solution)/shard_map/while/body/eval_jaxpr/all_gather | solution.py:91
  512.4 52.8 %reduce-scatter.39.cloned.1.call-start = ((), (), s32[]{:S(2)}) async-start(), calls=%async_computation.33 | async-start | bytes 2621440 | tf_op jit(solution)/shard_map/while/body/eval_jaxpr/reduce_scatter | solution.py:95
  516.4 80.9 %reduce-scatter.41.cloned.1.call-start = ((), (), s32[]{:S(2)}) async-start(), calls=%async_computation.34 | async-start | bytes 2621440 | tf_op jit(solution)/shard_map/while/body/eval_jaxpr/reduce_scatter | solution.py:343
  520.3 110.9 %reduce-scatter.37.cloned.1.call-start = ((), (), s32[]{:S(2)}) async-start(), calls=%async_computation.32 | async-start | bytes 2621440 | tf_op jit(solution)/shard_map/while/body/eval_jaxpr/reduce_scatter | solution.py:104
  573.0 58.2 %copy-start.1 = (bf16[2,256,512]{2,1,0:T(8,128)(2,1)S(1)}, bf16[2,256,512]{2,1,0:T(8,128)(2,1)}, u32[]{:S(2)}) copy-start(bf16[2,256,512]{2,1,0:T(8,128)(2,1)} %get-tuple-element.2074) | copy-start | bytes 1572868 | tf_op jit(solution)/shard_map/while
  573.0 58.2 %copy-start.40 = (f32[512]{0:T(512)S(1)}, f32[512]{0:T(512)}, u32[]{:S(2)}) copy-start(f32[512]{0:T(512)} %copy-done.39) | copy-start | bytes 6148 | tf_op jit(solution)/shard_map/while
  573.0 58.2 %copy-start.45 = (f32[256]{0:T(256)S(1)}, f32[256]{0:T(256)}, u32[]{:S(2)}) copy-start(f32[256]{0:T(256)} %copy-done.44) | copy-start | bytes 3076 | tf_op jit(solution)/shard_map/while
  573.0 59.5 %copy-start.69 = (f32[256]{0:T(256)S(1)}, f32[256]{0:T(256)}, u32[]{:S(2)}) copy-start(f32[256]{0:T(256)} %copy-done.68) | copy-start | bytes 3076 | tf_op jit(solution)/shard_map/while
  573.0 59.5 %copy-start.59 = (f32[256]{0:T(256)S(1)}, f32[256]{0:T(256)}, u32[]{:S(2)}) copy-start(f32[256]{0:T(256)} %copy-done.58) | copy-start | bytes 3076 | tf_op jit(solution)/shard_map/while
  573.1 60.8 %copy-start.85 = (f32[512]{0:T(512)}, f32[512]{0:T(512)S(1)}, u32[]{:S(2)}) copy-start(f32[512]{0:T(512)S(1)} %get-tuple-element.2068) | copy-start | bytes 6148 | tf_op jit(solution)/shard_map/while
  573.1 60.8 %copy-start.88 = (f32[512]{0:T(512)}, f32[512]{0:T(512)S(1)}, u32[]{:S(2)}) copy-start(f32[512]{0:T(512)S(1)} %get-tuple-element.2067) | copy-start | bytes 6148 | tf_op jit(solution)/shard_map/while
  636.2 96.5 %all-gather.12.cloned.1.call-start = ((), (), s32[]{:S(2)}) async-start(), calls=%async_computation.21 | async-start | bytes 1310720 | tf_op jit(solution)/shard_map/while/body/eval_jaxpr/all_gather | solution.py:87
  637.3 64.3 %copy-start.44 = (f32[256]{0:T(256)}, f32[256]{0:T(256)S(1)}, u32[]{:S(2)}) copy-start(f32[256]{0:T(256)S(1)} %broadcast_multiply_fusion.6) | copy-start | bytes 3076 | tf_op jit(solution)/shard_map/while
  638.5 63.1 %copy-start.58 = (f32[256]{0:T(256)}, f32[256]{0:T(256)S(1)}, u32[]{:S(2)}) copy-start(f32[256]{0:T(256)S(1)} %fusion.326) | copy-start | bytes 3076 | tf_op jit(solution)/shard_map/while
  669.6 109.1 %reduce-scatter.29.cloned.1.call-start = ((), (), s32[]{:S(2)}) async-start(), calls=%async_computation.22 | async-start | bytes 2621440 | tf_op jit(solution)/shard_map/while/body/eval_jaxpr/reduce_scatter | solution.py:95
  749.0 63.3 %copy-start.64 = (bf16[64,128]{1,0:T(8,128)(2,1)S(1)}, bf16[64,128]{1,0:T(8,128)(2,1)}, u32[]{:S(2)}) copy-start(bf16[64,128]{1,0:T(8,128)(2,1)} %get-tuple-element.2085) | copy-start | bytes 49156 | tf_op jit(solution)/shard_map/while
  749.0 93.8 %copy-start.50 = (bf16[2,64,128]{2,1,0:T(8,128)(2,1)S(1)}, bf16[2,64,128]{2,1,0:T(8,128)(2,1)}, u32[]{:S(2)}) copy-start(bf16[2,64,128]{2,1,0:T(8,128)(2,1)} %get-tuple-element.2087) | copy-start | bytes 98308 | tf_op jit(solution)/shard_map/while
  750.8 122.7 %all-gather.16.cloned.1.call-start = ((), (), s32[]{:S(2)}) async-start(), calls=%async_computation.24 | async-start | bytes 1310720 | tf_op jit(solution)/shard_map/while/body/eval_jaxpr/all_gather | solution.py:279
  751.7 123.8 %all-gather.14.cloned.1.call-start = ((), (), s32[]{:S(2)}) async-start(), calls=%async_computation.23 | async-start | bytes 1310720 | tf_op jit(solution)/shard_map/while/body/eval_jaxpr/all_gather | solution.py:278
  751.7 125.6 %copy-start.46 = (f32[512]{0:T(512)}, f32[512]{0:T(512)S(1)}, u32[]{:S(2)}) copy-start(f32[512]{0:T(512)S(1)} %convert_element_type.395) | copy-start | bytes 6148 | tf_op jit(solution)/shard_map/while
  779.9 97.8 %copy-start.54 = (f32[256]{0:T(256)}, f32[256]{0:T(256)S(1)}, u32[]{:S(2)}) copy-start(f32[256]{0:T(256)S(1)} %broadcast_multiply_fusion.7) | copy-start | bytes 3076 | tf_op jit(solution)/shard_map/while
  780.1 97.7 %copy-start.70 = (f32[256]{0:T(256)}, f32[256]{0:T(256)S(1)}, u32[]{:S(2)}) copy-start(f32[256]{0:T(256)S(1)} %multiply_reduce_fusion.14) | copy-start | bytes 3076 | tf_op jit(solution)/shard_map/while
  780.1 97.6 %copy-start.60 = (f32[256]{0:T(256)}, f32[256]{0:T(256)S(1)}, u32[]{:S(2)}) copy-start(f32[256]{0:T(256)S(1)} %fusion.332) | copy-start | bytes 3076 | tf_op jit(solution)/shard_map/while
  781.0 139.2 %reduce-scatter.31.cloned.1.call-start = ((), (), s32[]{:S(2)}) async-start(), calls=%async_computation.26 | async-start | bytes 2621440 | tf_op jit(solution)/shard_map/while/body/eval_jaxpr/reduce_scatter | solution.py:95
  886.9 69.4 %copy-start.37 = (bf16[512,64]{0,1:T(8,128)(2,1)S(1)}, bf16[512,64]{0,1:T(8,128)(2,1)}, u32[]{:S(2)}) copy-start(bf16[512,64]{0,1:T(8,128)(2,1)} %get-tuple-element.2081) | copy-start | bytes 196612 | tf_op jit(solution)/shard_map/while
  888.8 98.8 %all-gather.18.cloned.1.call-start = ((), (), s32[]{:S(2)}) async-start(), calls=%async_computation.25 | async-start | bytes 1310720 | tf_op jit(solution)/shard_map/while/body/eval_jaxpr/all_gather | solution.py:91
  890.3 100.7 %all-gather.20.cloned.1.call-start = ((), (), s32[]{:S(2)}) async-start(), calls=%async_computation.27 | async-start | bytes 1310720 | tf_op jit(solution)/shard_map/while/body/eval_jaxpr/all_gather | solution.py:87
  891.1 65.2 %copy-start.48 = (f32[512]{0:T(512)}, f32[512]{0:T(512)S(1)}, u32[]{:S(2)}) copy-start(f32[512]{0:T(512)S(1)} %convert_element_type.397) | copy-start | bytes 6148 | tf_op jit(solution)/shard_map/while
  922.6 108.5 %reduce-scatter.33.cloned.1.call-start = ((), (), s32[]{:S(2)}) async-start(), calls=%async_computation.28 | async-start | bytes 2621440 | tf_op jit(solution)/shard_map/while/body/eval_jaxpr/reduce_scatter | solution.py:104
  999.4 53.4 %all-gather.22.cloned.1.call-start = ((), (), s32[]{:S(2)}) async-start(), calls=%async_computation.29 | async-start | bytes 1310720 | tf_op jit(solution)/shard_map/while/body/eval_jaxpr/all_gather | solution.py:91
  1035.9 72.5 %reduce-scatter.35.cloned.1.call-start = ((), (), s32[]{:S(2)}) async-start(), calls=%async_computation.30 | async-start | bytes 2621440 | tf_op jit(solution)/shard_map/while/body/eval_jaxpr/reduce_scatter | solution.py:342
  1076.8 53.8 %all-gather.24.cloned.1.call-start = ((), (), s32[]{:S(2)}) async-start(), calls=%async_computation.31 | async-start | bytes 1310720 | tf_op jit(solution)/shard_map/while/body/eval_jaxpr/all_gather | solution.py:91
  1113.7 53.1 %reduce-scatter.39.cloned.1.call-start = ((), (), s32[]{:S(2)}) async-start(), calls=%async_computation.33 | async-start | bytes 2621440 | tf_op jit(solution)/shard_map/while/body/eval_jaxpr/reduce_scatter | solution.py:95
  1117.7 80.8 %reduce-scatter.41.cloned.1.call-start = ((), (), s32[]{:S(2)}) async-start(), calls=%async_computation.34 | async-start | bytes 2621440 | tf_op jit(solution)/shard_map/while/body/eval_jaxpr/reduce_scatter | solution.py:343
  1121.6 110.9 %reduce-scatter.37.cloned.1.call-start = ((), (), s32[]{:S(2)}) async-start(), calls=%async_computation.32 | async-start | bytes 2621440 | tf_op jit(solution)/shard_map/while/body/eval_jaxpr/reduce_scatter | solution.py:104
  1175.7 59.5 %copy-start.85 = (f32[512]{0:T(512)}, f32[512]{0:T(512)S(1)}, u32[]{:S(2)}) copy-start(f32[512]{0:T(512)S(1)} %get-tuple-element.2068) | copy-start | bytes 6148 | tf_op jit(solution)/shard_map/while
  1175.7 59.5 %copy-start.88 = (f32[512]{0:T(512)}, f32[512]{0:T(512)S(1)}, u32[]{:S(2)}) copy-start(f32[512]{0:T(512)S(1)} %get-tuple-element.2067) | copy-start | bytes 6148 | tf_op jit(solution)/shard_map/while
  1239.6 65.8 %reduce-scatter.19.cloned.1.call-start = ((), (), s32[]{:S(2)}) async-start(), calls=%async_computation.16 | async-start | bytes 294912 | tf_op jit(solution)/shard_map/reduce_scatter | solution.py:72
  1240.2 129.3 %reduce-scatter.17.cloned.1.call-start = ((), (), s32[]{:S(2)}) async-start(), calls=%async_computation.15 | async-start | bytes 294912 | tf_op jit(solution)/shard_map/reduce_scatter | solution.py:71
  1242.0 191.6 %reduce-scatter.23.cloned.1.call-start = ((), (), s32[]{:S(2)}) async-start(), calls=%async_computation.18 | async-start | bytes 294912 | tf_op jit(solution)/shard_map/reduce_scatter | solution.py:74
  1244.0 254.7 %reduce-scatter.21.cloned.1.call-start = ((), (), s32[]{:S(2)}) async-start(), calls=%async_computation.17 | async-start | bytes 589824 | tf_op jit(solution)/shard_map/reduce_scatter | solution.py:73
  1246.1 319.3 %reduce-scatter.15.cloned.1.call-start = ((), (), s32[]{:S(2)}) async-start(), calls=%async_computation.14 | async-start | bytes 884736 | tf_op jit(solution)/shard_map/reduce_scatter | solution.py:70
  1248.4 383.4 %reduce-scatter.25.cloned.1.call-start = ((), (), s32[]{:S(2)}) async-start(), calls=%async_computation.19 | async-start | bytes 1179648 | tf_op jit(solution)/shard_map/reduce_scatter | solution.py:75
  1249.2 449.5 %reduce-scatter.27.cloned.1.call-start = ((), (), s32[]{:S(2)}) async-start(), calls=%async_computation.20 | async-start | bytes 1179648 | tf_op jit(solution)/shard_map/reduce_scatter | solution.py:76
  (173 other events, 2961.0 us)
Sparse Core Ops, SparseCore 0:
  67.4 13.9 all-gather.11
  148.7 28.6 reduce-scatter.28
  179.0 16.7 all-gather.15
  197.3 16.7 all-gather.13
  287.5 31.3 reduce-scatter.30
  320.4 16.7 all-gather.17
  338.7 16.7 all-gather.19
  398.2 31.5 reduce-scatter.32
  434.8 16.7 all-gather.21
  475.7 31.3 reduce-scatter.34
  512.6 16.7 all-gather.23
  531.7 31.4 reduce-scatter.38
  565.9 31.4 reduce-scatter.40
  599.7 31.4 reduce-scatter.36
  669.7 13.0 all-gather.11
  751.0 27.7 reduce-scatter.28
  780.2 16.7 all-gather.15
  798.5 16.7 all-gather.13
  888.9 31.3 reduce-scatter.30
  921.7 16.7 all-gather.17
  940.0 16.7 all-gather.19
  999.5 31.5 reduce-scatter.32
  1036.1 16.7 all-gather.21
  1077.0 31.4 reduce-scatter.34
  1113.9 16.7 all-gather.23
  1133.0 31.4 reduce-scatter.38
  1167.0 31.4 reduce-scatter.40
  1201.0 31.4 reduce-scatter.36
Sparse Core Ops, SparseCore 1:
  1244.0 61.3 reduce-scatter.18
  1309.1 60.3 reduce-scatter.16
  1373.3 60.3 reduce-scatter.22
  1437.6 61.0 reduce-scatter.20
  1503.0 62.3 reduce-scatter.14
  1569.3 62.5 reduce-scatter.24
  1636.1 62.5 reduce-scatter.26
where the time goes:
time: 1710 us
  waiting for transfers between devices  795 us (46%)
  blocking collectives  527 us (31%)
  matrix products  166 us (10%)
  other arithmetic  91.1 us (5%)
  local copies, waits for them, and re-layouts  73.3 us (4%)
  loops' own time  36.5 us (2%)
    reduce_scatter x4, waiting for transfers between devices, input_grad(): lax.psum_scatter(grad_term(jnp.int32(0), own_rows * lax.axis_size('tensor...  117 us
    reduce_scatter x6, waiting for transfers between devices, branch_sum(): lax.psum_scatter(jnp.dot(mixture, weight, preferred_element_type=jnp.floa...  112 us
    all_gather x2, blocking collectives, gather_weights(): lax.all_gather(ffn_up, 'dp', axis=0, tiled=True)  67.2 us
    reduce_scatter x1, waiting for transfers between devices, reduce_grads(): lax.psum_scatter(grad_down, 'dp', scatter_dimension=1, tiled=True)  66.8 us
    reduce_scatter x1, waiting for transfers between devices, reduce_grads(): lax.psum_scatter(grad_qkv, 'dp', scatter_dimension=1, tiled=True)  66.6 us
    reduce_scatter x1, waiting for transfers between devices, reduce_grads(): lax.psum_scatter(grad_up, 'dp', scatter_dimension=0, tiled=True)  66.6 us
    reduce_scatter x1, waiting for transfers between devices, reduce_grads(): lax.psum_scatter(grad_pair, 'dp', scatter_dimension=1, tiled=True)  65 us
    reduce_scatter x1, waiting for transfers between devices, reduce_grads(): lax.psum_scatter(grad_cross, 'dp', scatter_dimension=1, tiled=True)  64.2 us
  transfers between devices with their start and end apart: 35, of which 23 were waited for; matrix products, arithmetic and copies ran while one was open for 9% of the time, Pallas kernels for 0%

commit v1 on v0

--- a/solution.py
+++ b/solution.py
@@ -7,6 +7,27 @@
 EPSILON = 1e-05
 MASKED = -1e30
 BLOCK_ROWS = 512
+
+
+def gather_around(shard, axis, dim):
+    size, mine, extent = (lax.axis_size(axis), lax.axis_index(axis), shard.shape[dim])
+    right = [(i, (i + 1) % size) for i in range(size)]
+    left = [(i, (i - 1) % size) for i in range(size)]
+    out = jnp.zeros((*shard.shape[:dim], size * extent, *shard.shape[dim + 1 :]), shard.dtype)
+    out = lax.dynamic_update_slice_in_dim(out, shard, mine * extent, axis=dim)
+    from_left = from_right = shard
+    middle = size // 2
+    for hop in range(1, middle + 1):
+        from_left = lax.ppermute(from_left, axis, right)
+        out = lax.dynamic_update_slice_in_dim(
+            out, from_left, (mine - hop) % size * extent, axis=dim
+        )
+        if hop < size - middle:
+            from_right = lax.ppermute(from_right, axis, left)
+            out = lax.dynamic_update_slice_in_dim(
+                out, from_right, (mine + hop) % size * extent, axis=dim
+            )
+    return out
 
 
 def layer_norm(values, gain_vec, bias_vec):
@@ -88,7 +109,7 @@
 
 
 def grad_rows(own_part):
-    return lax.all_gather(own_part, "tensor", axis=0, tiled=True)
+    return gather_around(own_part, "tensor", 0)
 
 
 def branch_sum(mixture, weight):

time: 1710 us -> 1660 us (0.971)
  waiting for transfers between devices: 795 us -> 726 us
  local copies, waits for them, and re-layouts: 73.3 us -> 98.4 us
  loops' own time: 36.5 us -> 13.2 us
    all_gather x6 -> x0, waiting for transfers between devices: 51.6 us -> none  [grad_rows(): return lax.all_gather(own_part, 'tensor', axis=0, tiled=True)]
    reduce_scatter x2, waiting for transfers between devices: 47 us -> 5 us  [advance(): lax.psum_scatter(back_memory, 'tensor', scatter_dimension=0, tiled=True)]
    ppermute x0 -> x18, waiting for transfers between devices: none -> 30.1 us  [the longest x12 30.1 us: gather_around(): from_left = lax.ppermute(from_left, axis, right)]
    dynamic_update_slice x0 -> x18, local copies, waits for them, and re-layouts: none -> 24.4 us  [the longest x12 16.3 us: gather_around(): lax.dynamic_update_slice_in_dim(out, from_left, (mine - hop) % size * ext...]
    another operation x1, loops' own time: 30.4 us -> 7.02 us  [body(): lax.scan(advance, accum_init, (inputs, memory, tgt_len, src_len, cotangent))]
  transfers between devices with their start and end apart: 35 -> 47, of which waited for: 23 -> 27; matrix products, arithmetic and copies ran while one was open for 9% -> 11% of each run, Pallas kernels for 0% -> 0%
where the time goes in v1:
time: 1660 us; the launch traced here: 1650 us
  waiting for transfers between devices  726 us (44%)
  blocking collectives  527 us (32%)
  matrix products  166 us (10%)
  local copies, waits for them, and re-layouts  98.4 us (6%)
  other arithmetic  92.5 us (6%)
  between operations  16.7 us (1%)
    reduce_scatter x4, waiting for transfers between devices, input_grad(): lax.psum_scatter(grad_term(jnp.int32(0), own_rows * lax.axis_size('tensor...  117 us
    reduce_scatter x6, waiting for transfers between devices, branch_sum(): lax.psum_scatter(jnp.dot(mixture, weight, preferred_element_type=jnp.floa...  115 us
    reduce_scatter x1, waiting for transfers between devices, reduce_grads(): lax.psum_scatter(grad_down, 'dp', scatter_dimension=1, tiled=True)  66.8 us
    reduce_scatter x1, waiting for transfers between devices, reduce_grads(): lax.psum_scatter(grad_qkv, 'dp', scatter_dimension=1, tiled=True)  66.5 us
    reduce_scatter x1, waiting for transfers between devices, reduce_grads(): lax.psum_scatter(grad_up, 'dp', scatter_dimension=0, tiled=True)  66.5 us
    all_gather x2, blocking collectives, gather_weights(): lax.all_gather(ffn_down, 'dp', axis=1, tiled=True)  66.4 us
    reduce_scatter x1, waiting for transfers between devices, reduce_grads(): lax.psum_scatter(grad_pair, 'dp', scatter_dimension=1, tiled=True)  65.1 us
    reduce_scatter x1, waiting for transfers between devices, reduce_grads(): lax.psum_scatter(grad_cross, 'dp', scatter_dimension=1, tiled=True)  64.2 us
  transfers between devices with their start and end apart: 47, of which 27 were waited for; matrix products, arithmetic and copies ran while one was open for 11% of the time, Pallas kernels for 0%

profile of v1, /device:TPU:0, one launch (start us, length us, event | category | flops | bytes accessed | tf_op | source)
XLA Modules:
  0.0 1653.6 jit_solution(10142993376522345186)
XLA Ops:
  8.2 1178.7 %while.159 = (s32[]{:T(128)}, f32[3,512,128]{1,2,0:T(8,128)}, f32[128,512]{1,0:T(8,128)}, f32[512,128]{1,0:T(8,128)}, f32[2,512,128]{1,2,0:T(8,128)}, /*index=5*...) while((s32[]{:T(128)}, f32[3,512,128]{1,2,0:T(8,128)}, ...), condition=%wide.region_40.41_spmd.clone, body=%wide.region_0.40_spmd.clone.sunk | while | flops 8421522944 | bytes 374971648 | solution.py:408
  18.0 23.9 %all-reduce.22 = (bf16[512]{0:T(512)(128)(2,1)S(1)}, bf16[512]{0:T(512)(128)(2,1)S(1)}, bf16[512]{0:T(512)(128)(2,1)S(1)}, bf16[512]{0:T(512)(128)(2,1)S(1)}, bf...) all-reduce(bf16[512]{0:T(512)(128)(2,1)S(1)} %dynamic-update-slice.18, ...), channel_id=1, replica_groups=mesh['dp'=8,'tensor'=4] {'dp'}, use_global_device_ids=true, to_apply=%add.1 | all-reduce | flops 3072 | bytes 12288 | tf_op jit(solution)/shard_map/while
  45.1 30.7 %all_gather.124 = bf16[128,512]{0,1:T(8,128)(2,1)S(1)} all-gather(bf16[128,64]{0,1:T(8,128)(2,1)} %get-tuple-element.2109), channel_id=1, replica_groups=mesh['dp'=8,'tensor'=4] {'dp'}, dimensions={1}, use_global_device_ids=true | all-gather | bytes 147456 | tf_op jit(solution)/shard_map/while/body/eval_jaxpr/all_gather | solution.py:60
  75.8 31.2 %all_gather.123 = bf16[3,512,128]{2,1,0:T(8,128)(2,1)S(1)} all-gather(bf16[3,64,128]{2,1,0:T(8,128)(2,1)} %get-tuple-element.2104), channel_id=1, replica_groups=mesh['dp'=8,'tensor'=4] {'dp'}, dimensions={1}, use_global_device_ids=true | all-gather | bytes 442368 | tf_op jit(solution)/shard_map/while/body/eval_jaxpr/all_gather | solution.py:59
  109.9 12.2 while.160
  126.0 27.9 %reduce-scatter.29.cloned.1.call-done = f32[256,512]{1,0:T(8,128)} async-done(((f32[1024,512]{1,0:T(8,128)}), f32[256,512]{1,0:T(8,128)}) %reduce-scatter.29.cloned.1.call-update) | async-done | bytes 524304 | tf_op jit(solution)/shard_map/while/body/eval_jaxpr/reduce_scatter | solution.py:116
  156.9 30.6 %all_gather.128 = bf16[128,512]{0,1:T(8,128)(2,1)S(1)} all-gather(bf16[128,64]{0,1:T(8,128)(2,1)S(1)} %copy-done.62), channel_id=1, replica_groups=mesh['dp'=8,'tensor'=4] {'dp'}, dimensions={1}, use_global_device_ids=true | all-gather | bytes 147456 | tf_op jit(solution)/shard_map/while/body/eval_jaxpr/all_gather | solution.py:63
  187.5 30.6 %all_gather.126 = bf16[512,128]{1,0:T(8,128)(2,1)S(1)} all-gather(bf16[64,128]{1,0:T(8,128)(2,1)S(1)} %copy-done.61), channel_id=1, replica_groups=mesh['dp'=8,'tensor'=4] {'dp'}, dimensions={0}, use_global_device_ids=true | all-gather | bytes 147456 | tf_op jit(solution)/shard_map/while/body/eval_jaxpr/all_gather | solution.py:61
  218.1 30.9 %all_gather.127 = bf16[2,512,128]{2,1,0:T(8,128)(2,1)S(1)} all-gather(bf16[2,64,128]{2,1,0:T(8,128)(2,1)S(1)} %copy-done.47), channel_id=1, replica_groups=mesh['dp'=8,'tensor'=4] {'dp'}, dimensions={1}, use_global_device_ids=true | all-gather | bytes 294912 | tf_op jit(solution)/shard_map/while/body/eval_jaxpr/all_gather | solution.py:62
  253.3 8.1 while.161
  265.5 30.2 %reduce-scatter.31.cloned.1.call-done = f32[256,512]{1,0:T(8,128)} async-done(((f32[1024,512]{1,0:T(8,128)}), f32[256,512]{1,0:T(8,128)}) %reduce-scatter.31.cloned.1.call-update) | async-done | bytes 524304 | tf_op jit(solution)/shard_map/while/body/eval_jaxpr/reduce_scatter | solution.py:116
  303.1 31.4 %all_gather.130 = bf16[512,512]{1,0:T(8,128)(2,1)S(1)} all-gather(bf16[64,512]{1,0:T(8,128)(2,1)S(1)} %copy-done.38), channel_id=1, replica_groups=mesh['dp'=8,'tensor'=4] {'dp'}, dimensions={0}, use_global_device_ids=true | all-gather | bytes 589824 | tf_op jit(solution)/shard_map/while/body/eval_jaxpr/all_gather | solution.py:64
  334.6 33.2 %all_gather.131 = bf16[512,512]{0,1:T(8,128)(2,1)} all-gather(bf16[512,64]{0,1:T(8,128)(2,1)S(1)} %copy-done.37), channel_id=1, replica_groups=mesh['dp'=8,'tensor'=4] {'dp'}, dimensions={1}, use_global_device_ids=true | all-gather | bytes 589824 | tf_op jit(solution)/shard_map/while/body/eval_jaxpr/all_gather | solution.py:65
  374.7 3.9 fusion.337
  381.9 31.8 %reduce-scatter.33.cloned.1.call-done = f32[256,512]{1,0:T(8,128)} async-done(((f32[1024,512]{1,0:T(8,128)}), f32[256,512]{1,0:T(8,128)}) %reduce-scatter.33.cloned.1.call-update) | async-done | bytes 524304 | tf_op jit(solution)/shard_map/while/body/eval_jaxpr/reduce_scatter | solution.py:125
  420.8 6.6 collective-permute-done.3
  431.0 2.7 collective-permute-done.5
  441.7 13.5 while.162
  456.6 2.8 fusion.340
  459.5 3.8 fusion.346
  463.4 27.3 %reduce-scatter.35.cloned.1.call-done = f32[256,512]{1,0:T(8,128)} async-done(((f32[1024,512]{1,0:T(8,128)}), f32[256,512]{1,0:T(8,128)}) %reduce-scatter.35.cloned.1.call-update) | async-done | bytes 524304 | tf_op jit(solution)/shard_map/while/body/eval_jaxpr/reduce_scatter | solution.py:363
  500.1 3.6 collective-permute-done.6
  513.3 21.8 %while.163 = (s32[]{:T(128)}, f32[1024,2,64]{0,2,1:T(8,128)S(1)}, f32[1024,2,64]{0,2,1:T(8,128)}, bf16[2,512,2,64]{1,3,2,0:T(8,128)(2,1)}, bf16[2,512,2,64]{1,3,...) while((s32[]{:T(128)}, f32[1024,2,64]{0,2,1:T(8,128)S(1)}, ...), condition=%wide.region_28.28_spmd.clone, body=%wide.region_26.27_spmd.clone.sunk | while | flops 688587264 | bytes 37259468 | solution.py:212
  526.8 3.2 fusion.384
  540.1 3.0 convolution_add_fusion.13
  543.2 4.2 convolution_add_fusion.14
  555.5 3.3 reduce-scatter.41.cloned.1.call-done
  563.0 2.9 fusion.342
  565.9 26.8 %reduce-scatter.37.cloned.1.call-done = f32[256,512]{1,0:T(8,128)} async-done(((f32[1024,512]{1,0:T(8,128)}), f32[256,512]{1,0:T(8,128)}) %reduce-scatter.37.cloned.1.call-update) | async-done | bytes 524304 | tf_op jit(solution)/shard_map/while/body/eval_jaxpr/reduce_scatter | solution.py:125
  607.3 22.2 %all-reduce.22 = (bf16[512]{0:T(512)(128)(2,1)S(1)}, bf16[512]{0:T(512)(128)(2,1)S(1)}, bf16[512]{0:T(512)(128)(2,1)S(1)}, bf16[512]{0:T(512)(128)(2,1)S(1)}, bf...) all-reduce(bf16[512]{0:T(512)(128)(2,1)S(1)} %dynamic-update-slice.18, ...), channel_id=1, replica_groups=mesh['dp'=8,'tensor'=4] {'dp'}, use_global_device_ids=true, to_apply=%add.1 | all-reduce | flops 3072 | bytes 12288 | tf_op jit(solution)/shard_map/while
  632.6 30.7 %all_gather.124 = bf16[128,512]{0,1:T(8,128)(2,1)S(1)} all-gather(bf16[128,64]{0,1:T(8,128)(2,1)} %get-tuple-element.2109), channel_id=1, replica_groups=mesh['dp'=8,'tensor'=4] {'dp'}, dimensions={1}, use_global_device_ids=true | all-gather | bytes 147456 | tf_op jit(solution)/shard_map/while/body/eval_jaxpr/all_gather | solution.py:60
  663.4 31.2 %all_gather.123 = bf16[3,512,128]{2,1,0:T(8,128)(2,1)S(1)} all-gather(bf16[3,64,128]{2,1,0:T(8,128)(2,1)} %get-tuple-element.2104), channel_id=1, replica_groups=mesh['dp'=8,'tensor'=4] {'dp'}, dimensions={1}, use_global_device_ids=true | all-gather | bytes 442368 | tf_op jit(solution)/shard_map/while/body/eval_jaxpr/all_gather | solution.py:59
  697.5 12.2 while.160
  713.5 27.0 %reduce-scatter.29.cloned.1.call-done = f32[256,512]{1,0:T(8,128)} async-done(((f32[1024,512]{1,0:T(8,128)}), f32[256,512]{1,0:T(8,128)}) %reduce-scatter.29.cloned.1.call-update) | async-done | bytes 524304 | tf_op jit(solution)/shard_map/while/body/eval_jaxpr/reduce_scatter | solution.py:116
  743.5 30.6 %all_gather.128 = bf16[128,512]{0,1:T(8,128)(2,1)S(1)} all-gather(bf16[128,64]{0,1:T(8,128)(2,1)S(1)} %copy-done.62), channel_id=1, replica_groups=mesh['dp'=8,'tensor'=4] {'dp'}, dimensions={1}, use_global_device_ids=true | all-gather | bytes 147456 | tf_op jit(solution)/shard_map/while/body/eval_jaxpr/all_gather | solution.py:63
  774.1 30.6 %all_gather.126 = bf16[512,128]{1,0:T(8,128)(2,1)S(1)} all-gather(bf16[64,128]{1,0:T(8,128)(2,1)S(1)} %copy-done.61), channel_id=1, replica_groups=mesh['dp'=8,'tensor'=4] {'dp'}, dimensions={0}, use_global_device_ids=true | all-gather | bytes 147456 | tf_op jit(solution)/shard_map/while/body/eval_jaxpr/all_gather | solution.py:61
  804.7 30.9 %all_gather.127 = bf16[2,512,128]{2,1,0:T(8,128)(2,1)S(1)} all-gather(bf16[2,64,128]{2,1,0:T(8,128)(2,1)S(1)} %copy-done.47), channel_id=1, replica_groups=mesh['dp'=8,'tensor'=4] {'dp'}, dimensions={1}, use_global_device_ids=true | all-gather | bytes 294912 | tf_op jit(solution)/shard_map/while/body/eval_jaxpr/all_gather | solution.py:62
  839.9 8.1 while.161
  852.1 30.2 %reduce-scatter.31.cloned.1.call-done = f32[256,512]{1,0:T(8,128)} async-done(((f32[1024,512]{1,0:T(8,128)}), f32[256,512]{1,0:T(8,128)}) %reduce-scatter.31.cloned.1.call-update) | async-done | bytes 524304 | tf_op jit(solution)/shard_map/while/body/eval_jaxpr/reduce_scatter | solution.py:116
  889.8 31.5 %all_gather.130 = bf16[512,512]{1,0:T(8,128)(2,1)S(1)} all-gather(bf16[64,512]{1,0:T(8,128)(2,1)S(1)} %copy-done.38), channel_id=1, replica_groups=mesh['dp'=8,'tensor'=4] {'dp'}, dimensions={0}, use_global_device_ids=true | all-gather | bytes 589824 | tf_op jit(solution)/shard_map/while/body/eval_jaxpr/all_gather | solution.py:64
  921.3 33.2 %all_gather.131 = bf16[512,512]{0,1:T(8,128)(2,1)} all-gather(bf16[512,64]{0,1:T(8,128)(2,1)S(1)} %copy-done.37), channel_id=1, replica_groups=mesh['dp'=8,'tensor'=4] {'dp'}, dimensions={1}, use_global_device_ids=true | all-gather | bytes 589824 | tf_op jit(solution)/shard_map/while/body/eval_jaxpr/all_gather | solution.py:65
  961.4 3.9 fusion.337
  968.6 31.8 %reduce-scatter.33.cloned.1.call-done = f32[256,512]{1,0:T(8,128)} async-done(((f32[1024,512]{1,0:T(8,128)}), f32[256,512]{1,0:T(8,128)}) %reduce-scatter.33.cloned.1.call-update) | async-done | bytes 524304 | tf_op jit(solution)/shard_map/while/body/eval_jaxpr/reduce_scatter | solution.py:125
  1007.5 6.6 collective-permute-done.3
  1028.7 13.5 while.162
  1043.5 2.8 fusion.340
  1046.4 3.8 fusion.346
  1050.3 27.3 %reduce-scatter.35.cloned.1.call-done = f32[256,512]{1,0:T(8,128)} async-done(((f32[1024,512]{1,0:T(8,128)}), f32[256,512]{1,0:T(8,128)}) %reduce-scatter.35.cloned.1.call-update) | async-done | bytes 524304 | tf_op jit(solution)/shard_map/while/body/eval_jaxpr/reduce_scatter | solution.py:363
  1087.0 3.6 collective-permute-done.6
  1100.2 21.8 %while.163 = (s32[]{:T(128)}, f32[1024,2,64]{0,2,1:T(8,128)S(1)}, f32[1024,2,64]{0,2,1:T(8,128)}, bf16[2,512,2,64]{1,3,2,0:T(8,128)(2,1)}, bf16[2,512,2,64]{1,3,...) while((s32[]{:T(128)}, f32[1024,2,64]{0,2,1:T(8,128)S(1)}, ...), condition=%wide.region_28.28_spmd.clone, body=%wide.region_26.27_spmd.clone.sunk | while | flops 688587264 | bytes 37259468 | solution.py:212
  1113.7 3.2 fusion.384
  1127.1 3.3 convolution_add_fusion.13
  1130.4 4.5 convolution_add_fusion.14
  1150.0 3.1 fusion.342
  1153.1 26.6 %reduce-scatter.37.cloned.1.call-done = f32[256,512]{1,0:T(8,128)} async-done(((f32[1024,512]{1,0:T(8,128)}), f32[256,512]{1,0:T(8,128)}) %reduce-scatter.37.cloned.1.call-update) | async-done | bytes 524304 | tf_op jit(solution)/shard_map/while/body/eval_jaxpr/reduce_scatter | solution.py:125
  1199.3 37.1 %all-reduce.19 = (f32[512]{0:T(512)S(1)}, f32[512]{0:T(512)S(1)}, f32[512]{0:T(512)S(1)}, f32[512]{0:T(512)S(1)}, f32[512]{0:T(512)S(1)}, /*index=5*/f32[512]{0:T(512)S(1)}) all-reduce(f32[512]{0:T(512)S(1)} %copy-done.92, f32[512]{0:T(512)S(1)} %copy-done.89, ...), channel_id=17, replica_groups=mesh['dp'=8,'tensor'=4] {'dp'}, use_global_device_ids=true, to_apply=%region_48.49.clone | all-reduce | flops 3072 | bytes 24576
  1236.8 6.4 all-reduce.20
  1243.2 9.4 reduce-scatter.19.cloned.1.call-done
  1252.7 64.1 %reduce-scatter.17.cloned.1.call-done = f32[128,64]{0,1:T(8,128)} async-done(((f32[128,512]{0,1:T(8,128)}), f32[128,64]{0,1:T(8,128)}) %reduce-scatter.17.cloned.1.call-update) | async-done | bytes 32784 | tf_op jit(solution)/shard_map/reduce_scatter | solution.py:92
  1316.8 64.2 %reduce-scatter.23.cloned.1.call-done = f32[128,64]{0,1:T(8,128)} async-done(((f32[128,512]{0,1:T(8,128)}), f32[128,64]{0,1:T(8,128)}) %reduce-scatter.23.cloned.1.call-update) | async-done | bytes 32784 | tf_op jit(solution)/shard_map/reduce_scatter | solution.py:95
  1381.0 65.1 %reduce-scatter.21.cloned.1.call-done = f32[2,64,128]{2,1,0:T(8,128)} async-done(((f32[2,512,128]{2,1,0:T(8,128)}), f32[2,64,128]{2,1,0:T(8,128)}) %reduce-scatter.21.cloned.1.call-update) | async-done | bytes 65552 | tf_op jit(solution)/shard_map/reduce_scatter | solution.py:94
  1446.1 66.5 %reduce-scatter.15.cloned.1.call-done = f32[3,64,128]{2,1,0:T(8,128)} async-done(((f32[3,512,128]{2,1,0:T(8,128)}), f32[3,64,128]{2,1,0:T(8,128)}) %reduce-scatter.15.cloned.1.call-update) | async-done | bytes 98320 | tf_op jit(solution)/shard_map/reduce_scatter | solution.py:91
  1512.6 66.5 %reduce-scatter.25.cloned.1.call-done = f32[64,512]{1,0:T(8,128)} async-done(((f32[512,512]{1,0:T(8,128)}), f32[64,512]{1,0:T(8,128)}) %reduce-scatter.25.cloned.1.call-update) | async-done | bytes 131088 | tf_op jit(solution)/shard_map/reduce_scatter | solution.py:96
  1579.1 66.8 %reduce-scatter.27.cloned.1.call-done = f32[512,64]{0,1:T(8,128)} async-done(((f32[512,512]{0,1:T(8,128)}), f32[512,64]{0,1:T(8,128)}) %reduce-scatter.27.cloned.1.call-update) | async-done | bytes 131088 | tf_op jit(solution)/shard_map/reduce_scatter | solution.py:97
  (890 shorter events, 332.3 us)
Async XLA Ops:
  8.6 98.4 %all-gather.9.cloned.1.call-start = ((), (), s32[]{:S(2)}) async-start(), calls=%async_computation.21 | async-start | bytes 1310720 | tf_op jit(solution)/shard_map/while/body/eval_jaxpr/all_gather | solution.py:108
  9.8 66.0 %copy-start.42 = (f32[256]{0:T(256)}, f32[256]{0:T(256)S(1)}, u32[]{:S(2)}) copy-start(f32[256]{0:T(256)S(1)} %broadcast_multiply_fusion.6) | copy-start | bytes 3076 | tf_op jit(solution)/shard_map/while
  11.0 64.8 %copy-start.55 = (f32[256]{0:T(256)}, f32[256]{0:T(256)S(1)}, u32[]{:S(2)}) copy-start(f32[256]{0:T(256)S(1)} %fusion.324) | copy-start | bytes 3076 | tf_op jit(solution)/shard_map/while
  43.8 110.1 %reduce-scatter.29.cloned.1.call-start = ((), (), s32[]{:S(2)}) async-start(), calls=%async_computation.22 | async-start | bytes 2621440 | tf_op jit(solution)/shard_map/while/body/eval_jaxpr/reduce_scatter | solution.py:116
  123.2 64.3 %copy-start.61 = (bf16[64,128]{1,0:T(8,128)(2,1)S(1)}, bf16[64,128]{1,0:T(8,128)(2,1)}, u32[]{:S(2)}) copy-start(bf16[64,128]{1,0:T(8,128)(2,1)} %get-tuple-element.2112) | copy-start | bytes 49156 | tf_op jit(solution)/shard_map/while
  123.2 94.9 %copy-start.47 = (bf16[2,64,128]{2,1,0:T(8,128)(2,1)S(1)}, bf16[2,64,128]{2,1,0:T(8,128)(2,1)}, u32[]{:S(2)}) copy-start(bf16[2,64,128]{2,1,0:T(8,128)(2,1)} %get-tuple-element.2114) | copy-start | bytes 98308 | tf_op jit(solution)/shard_map/while
  125.1 123.9 %all-gather.13.cloned.1.call-start = ((), (), s32[]{:S(2)}) async-start(), calls=%async_computation.24 | async-start | bytes 1310720 | tf_op jit(solution)/shard_map/while/body/eval_jaxpr/all_gather | solution.py:300
  125.9 125.0 %all-gather.11.cloned.1.call-start = ((), (), s32[]{:S(2)}) async-start(), calls=%async_computation.23 | async-start | bytes 1310720 | tf_op jit(solution)/shard_map/while/body/eval_jaxpr/all_gather | solution.py:299
  125.9 123.1 %copy-start.44 = (f32[512]{0:T(512)}, f32[512]{0:T(512)S(1)}, u32[]{:S(2)}) copy-start(f32[512]{0:T(512)S(1)} %convert_element_type.393) | copy-start | bytes 6148 | tf_op jit(solution)/shard_map/while
  155.1 98.1 %copy-start.48 = (f32[256]{0:T(256)}, f32[256]{0:T(256)S(1)}, u32[]{:S(2)}) copy-start(f32[256]{0:T(256)S(1)} %broadcast_multiply_fusion.7) | copy-start | bytes 3076 | tf_op jit(solution)/shard_map/while
  155.3 97.9 %copy-start.65 = (f32[256]{0:T(256)}, f32[256]{0:T(256)S(1)}, u32[]{:S(2)}) copy-start(f32[256]{0:T(256)S(1)} %multiply_reduce_fusion.14) | copy-start | bytes 3076 | tf_op jit(solution)/shard_map/while
  155.3 97.9 %copy-start.57 = (f32[256]{0:T(256)}, f32[256]{0:T(256)S(1)}, u32[]{:S(2)}) copy-start(f32[256]{0:T(256)S(1)} %fusion.330) | copy-start | bytes 3076 | tf_op jit(solution)/shard_map/while
  156.3 139.4 %reduce-scatter.31.cloned.1.call-start = ((), (), s32[]{:S(2)}) async-start(), calls=%async_computation.25 | async-start | bytes 2621440 | tf_op jit(solution)/shard_map/while/body/eval_jaxpr/reduce_scatter | solution.py:116
  264.2 70.4 %copy-start.37 = (bf16[512,64]{0,1:T(8,128)(2,1)S(1)}, bf16[512,64]{0,1:T(8,128)(2,1)}, u32[]{:S(2)}) copy-start(bf16[512,64]{0,1:T(8,128)(2,1)} %get-tuple-element.2108) | copy-start | bytes 196612 | tf_op jit(solution)/shard_map/while
  264.2 108.6 %all-gather.15.cloned.1.call-start = ((), (), s32[]{:S(2)}) async-start(), calls=%async_computation.26 | async-start | bytes 1310720 | tf_op jit(solution)/shard_map/while/body/eval_jaxpr/all_gather | solution.py:108
  299.7 113.9 %reduce-scatter.33.cloned.1.call-start = ((), (), s32[]{:S(2)}) async-start(), calls=%async_computation.27 | async-start | bytes 2621440 | tf_op jit(solution)/shard_map/while/body/eval_jaxpr/reduce_scatter | solution.py:125
  301.4 33.2 %collective-permute-start = (bf16[256,512]{1,0:T(8,128)(2,1)}, bf16[256,512]{1,0:T(8,128)(2,1)}, u32[]{:S(2)}, u32[]{:S(2)}) collective-permute-start(bf16[256,512]{1,0:T(8,128)(2,1)} %get-tuple-element.1760), channel_id=1, source_target_pairs={{0,1},{1,2},{2,3},{3,0},{4,5},{5,6},{6,7},{7,4},{8,9},{9,10},{10,1... | collective-permute-start | bytes 786440 | tf_op jit(solution)/shard_map/while/body/eval_jaxpr/ppermute | solution.py:21
  301.4 68.1 %collective-permute-start.1 = (bf16[256,512]{1,0:T(8,128)(2,1)}, bf16[256,512]{1,0:T(8,128)(2,1)}, u32[]{:S(2)}, u32[]{:S(2)}) collective-permute-start(bf16[256,512]{1,0:T(8,128)(2,1)} %get-tuple-element.1760), channel_id=1, source_target_pairs={{0,3},{1,0},{2,1},{3,2},{4,7},{5,4},{6,5},{7,6},{8,11},{9,8},{10,9... | collective-permute-start | bytes 786440 | tf_op jit(solution)/shard_map/while/body/eval_jaxpr/ppermute | solution.py:26
  334.5 36.6 %collective-permute-start.2 = (bf16[256,512]{1,0:T(8,128)(2,1)}, bf16[256,512]{1,0:T(8,128)(2,1)}, u32[]{:S(2)}, u32[]{:S(2)}) collective-permute-start(bf16[256,512]{1,0:T(8,128)(2,1)} %collective-permute-done), channel_id=1, source_target_pairs={{0,1},{1,2},{2,3},{3,0},{4,5},{5,6},{6,7},{7,4},{8,9},{9,10},{10,1... | collective-permute-start | bytes 786440 | tf_op jit(solution)/shard_map/while/body/eval_jaxpr/ppermute | solution.py:21
  381.8 108.9 %reduce-scatter.35.cloned.1.call-start = ((), (), s32[]{:S(2)}) async-start(), calls=%async_computation.28 | async-start | bytes 2621440 | tf_op jit(solution)/shard_map/while/body/eval_jaxpr/reduce_scatter | solution.py:363
  419.0 8.4 collective-permute-start.3
  419.0 10.3 collective-permute-start.4
  427.4 6.3 collective-permute-start.5
  459.4 88.1 %reduce-scatter.39.cloned.1.call-start = ((), (), s32[]{:S(2)}) async-start(), calls=%async_computation.30 | async-start | bytes 2621440 | tf_op jit(solution)/shard_map/while/body/eval_jaxpr/reduce_scatter | solution.py:116
  463.3 95.4 %reduce-scatter.41.cloned.1.call-start = ((), (), s32[]{:S(2)}) async-start(), calls=%async_computation.31 | async-start | bytes 2621440 | tf_op jit(solution)/shard_map/while/body/eval_jaxpr/reduce_scatter | solution.py:364
  497.1 6.6 collective-permute-start.6
  498.3 8.5 collective-permute-start.7
  503.7 5.8 collective-permute-start.8
  505.6 87.1 %reduce-scatter.37.cloned.1.call-start = ((), (), s32[]{:S(2)}) async-start(), calls=%async_computation.29 | async-start | bytes 2621440 | tf_op jit(solution)/shard_map/while/body/eval_jaxpr/reduce_scatter | solution.py:125
  597.9 96.6 %all-gather.9.cloned.1.call-start = ((), (), s32[]{:S(2)}) async-start(), calls=%async_computation.21 | async-start | bytes 1310720 | tf_op jit(solution)/shard_map/while/body/eval_jaxpr/all_gather | solution.py:108
  599.1 64.3 %copy-start.42 = (f32[256]{0:T(256)}, f32[256]{0:T(256)S(1)}, u32[]{:S(2)}) copy-start(f32[256]{0:T(256)S(1)} %broadcast_multiply_fusion.6) | copy-start | bytes 3076 | tf_op jit(solution)/shard_map/while
  631.3 109.1 %reduce-scatter.29.cloned.1.call-start = ((), (), s32[]{:S(2)}) async-start(), calls=%async_computation.22 | async-start | bytes 2621440 | tf_op jit(solution)/shard_map/while/body/eval_jaxpr/reduce_scatter | solution.py:116
  710.8 63.3 %copy-start.61 = (bf16[64,128]{1,0:T(8,128)(2,1)S(1)}, bf16[64,128]{1,0:T(8,128)(2,1)}, u32[]{:S(2)}) copy-start(bf16[64,128]{1,0:T(8,128)(2,1)} %get-tuple-element.2112) | copy-start | bytes 49156 | tf_op jit(solution)/shard_map/while
  710.8 93.9 %copy-start.47 = (bf16[2,64,128]{2,1,0:T(8,128)(2,1)S(1)}, bf16[2,64,128]{2,1,0:T(8,128)(2,1)}, u32[]{:S(2)}) copy-start(bf16[2,64,128]{2,1,0:T(8,128)(2,1)} %get-tuple-element.2114) | copy-start | bytes 98308 | tf_op jit(solution)/shard_map/while
  712.6 123.0 %all-gather.13.cloned.1.call-start = ((), (), s32[]{:S(2)}) async-start(), calls=%async_computation.24 | async-start | bytes 1310720 | tf_op jit(solution)/shard_map/while/body/eval_jaxpr/all_gather | solution.py:300
  713.4 124.1 %all-gather.11.cloned.1.call-start = ((), (), s32[]{:S(2)}) async-start(), calls=%async_computation.23 | async-start | bytes 1310720 | tf_op jit(solution)/shard_map/while/body/eval_jaxpr/all_gather | solution.py:299
  713.5 122.1 %copy-start.44 = (f32[512]{0:T(512)}, f32[512]{0:T(512)S(1)}, u32[]{:S(2)}) copy-start(f32[512]{0:T(512)S(1)} %convert_element_type.393) | copy-start | bytes 6148 | tf_op jit(solution)/shard_map/while
  741.7 98.2 %copy-start.48 = (f32[256]{0:T(256)}, f32[256]{0:T(256)S(1)}, u32[]{:S(2)}) copy-start(f32[256]{0:T(256)S(1)} %broadcast_multiply_fusion.7) | copy-start | bytes 3076 | tf_op jit(solution)/shard_map/while
  741.9 98.0 %copy-start.65 = (f32[256]{0:T(256)}, f32[256]{0:T(256)S(1)}, u32[]{:S(2)}) copy-start(f32[256]{0:T(256)S(1)} %multiply_reduce_fusion.14) | copy-start | bytes 3076 | tf_op jit(solution)/shard_map/while
  741.9 98.0 %copy-start.57 = (f32[256]{0:T(256)}, f32[256]{0:T(256)S(1)}, u32[]{:S(2)}) copy-start(f32[256]{0:T(256)S(1)} %fusion.330) | copy-start | bytes 3076 | tf_op jit(solution)/shard_map/while
  742.8 139.4 %reduce-scatter.31.cloned.1.call-start = ((), (), s32[]{:S(2)}) async-start(), calls=%async_computation.25 | async-start | bytes 2621440 | tf_op jit(solution)/shard_map/while/body/eval_jaxpr/reduce_scatter | solution.py:116
  850.8 70.5 %copy-start.37 = (bf16[512,64]{0,1:T(8,128)(2,1)S(1)}, bf16[512,64]{0,1:T(8,128)(2,1)}, u32[]{:S(2)}) copy-start(bf16[512,64]{0,1:T(8,128)(2,1)} %get-tuple-element.2108) | copy-start | bytes 196612 | tf_op jit(solution)/shard_map/while
  850.9 108.6 %all-gather.15.cloned.1.call-start = ((), (), s32[]{:S(2)}) async-start(), calls=%async_computation.26 | async-start | bytes 1310720 | tf_op jit(solution)/shard_map/while/body/eval_jaxpr/all_gather | solution.py:108
  886.4 114.0 %reduce-scatter.33.cloned.1.call-start = ((), (), s32[]{:S(2)}) async-start(), calls=%async_computation.27 | async-start | bytes 2621440 | tf_op jit(solution)/shard_map/while/body/eval_jaxpr/reduce_scatter | solution.py:125
  888.0 33.2 %collective-permute-start = (bf16[256,512]{1,0:T(8,128)(2,1)}, bf16[256,512]{1,0:T(8,128)(2,1)}, u32[]{:S(2)}, u32[]{:S(2)}) collective-permute-start(bf16[256,512]{1,0:T(8,128)(2,1)} %get-tuple-element.1760), channel_id=1, source_target_pairs={{0,1},{1,2},{2,3},{3,0},{4,5},{5,6},{6,7},{7,4},{8,9},{9,10},{10,1... | collective-permute-start | bytes 786440 | tf_op jit(solution)/shard_map/while/body/eval_jaxpr/ppermute | solution.py:21
  888.0 68.1 %collective-permute-start.1 = (bf16[256,512]{1,0:T(8,128)(2,1)}, bf16[256,512]{1,0:T(8,128)(2,1)}, u32[]{:S(2)}, u32[]{:S(2)}) collective-permute-start(bf16[256,512]{1,0:T(8,128)(2,1)} %get-tuple-element.1760), channel_id=1, source_target_pairs={{0,3},{1,0},{2,1},{3,2},{4,7},{5,4},{6,5},{7,6},{8,11},{9,8},{10,9... | collective-permute-start | bytes 786440 | tf_op jit(solution)/shard_map/while/body/eval_jaxpr/ppermute | solution.py:26
  921.3 36.6 %collective-permute-start.2 = (bf16[256,512]{1,0:T(8,128)(2,1)}, bf16[256,512]{1,0:T(8,128)(2,1)}, u32[]{:S(2)}, u32[]{:S(2)}) collective-permute-start(bf16[256,512]{1,0:T(8,128)(2,1)} %collective-permute-done), channel_id=1, source_target_pairs={{0,1},{1,2},{2,3},{3,0},{4,5},{5,6},{6,7},{7,4},{8,9},{9,10},{10,1... | collective-permute-start | bytes 786440 | tf_op jit(solution)/shard_map/while/body/eval_jaxpr/ppermute | solution.py:21
  968.5 109.1 %reduce-scatter.35.cloned.1.call-start = ((), (), s32[]{:S(2)}) async-start(), calls=%async_computation.28 | async-start | bytes 2621440 | tf_op jit(solution)/shard_map/while/body/eval_jaxpr/reduce_scatter | solution.py:363
  1005.8 8.4 collective-permute-start.3
  1005.8 10.5 collective-permute-start.4
  1014.1 6.5 collective-permute-start.5
  1046.4 88.7 %reduce-scatter.39.cloned.1.call-start = ((), (), s32[]{:S(2)}) async-start(), calls=%async_computation.30 | async-start | bytes 2621440 | tf_op jit(solution)/shard_map/while/body/eval_jaxpr/reduce_scatter | solution.py:116
  1050.3 95.4 %reduce-scatter.41.cloned.1.call-start = ((), (), s32[]{:S(2)}) async-start(), calls=%async_computation.31 | async-start | bytes 2621440 | tf_op jit(solution)/shard_map/while/body/eval_jaxpr/reduce_scatter | solution.py:364
  1084.0 6.6 collective-permute-start.6
  1085.2 8.2 collective-permute-start.7
  1090.6 5.8 collective-permute-start.8
  1092.5 87.2 %reduce-scatter.37.cloned.1.call-start = ((), (), s32[]{:S(2)}) async-start(), calls=%async_computation.29 | async-start | bytes 2621440 | tf_op jit(solution)/shard_map/while/body/eval_jaxpr/reduce_scatter | solution.py:125
  1186.9 65.8 %reduce-scatter.19.cloned.1.call-start = ((), (), s32[]{:S(2)}) async-start(), calls=%async_computation.16 | async-start | bytes 294912 | tf_op jit(solution)/shard_map/reduce_scatter | solution.py:93
  1187.5 129.3 %reduce-scatter.17.cloned.1.call-start = ((), (), s32[]{:S(2)}) async-start(), calls=%async_computation.15 | async-start | bytes 294912 | tf_op jit(solution)/shard_map/reduce_scatter | solution.py:92
  1189.4 191.6 %reduce-scatter.23.cloned.1.call-start = ((), (), s32[]{:S(2)}) async-start(), calls=%async_computation.18 | async-start | bytes 294912 | tf_op jit(solution)/shard_map/reduce_scatter | solution.py:95
  1191.3 254.8 %reduce-scatter.21.cloned.1.call-start = ((), (), s32[]{:S(2)}) async-start(), calls=%async_computation.17 | async-start | bytes 589824 | tf_op jit(solution)/shard_map/reduce_scatter | solution.py:94
  1193.4 319.2 %reduce-scatter.15.cloned.1.call-start = ((), (), s32[]{:S(2)}) async-start(), calls=%async_computation.14 | async-start | bytes 884736 | tf_op jit(solution)/shard_map/reduce_scatter | solution.py:91
  1195.8 383.4 %reduce-scatter.25.cloned.1.call-start = ((), (), s32[]{:S(2)}) async-start(), calls=%async_computation.19 | async-start | bytes 1179648 | tf_op jit(solution)/shard_map/reduce_scatter | solution.py:96
  1196.5 449.4 %reduce-scatter.27.cloned.1.call-start = ((), (), s32[]{:S(2)}) async-start(), calls=%async_computation.20 | async-start | bytes 1179648 | tf_op jit(solution)/shard_map/reduce_scatter | solution.py:97
  (181 other events, 3039.4 us)
Sparse Core Ops, SparseCore 0:
  43.9 13.9 all-gather.8
  125.2 28.6 reduce-scatter.28
  155.5 16.7 all-gather.12
  173.8 16.7 all-gather.10
  264.4 31.2 reduce-scatter.30
  299.9 17.3 all-gather.14
  381.9 31.6 reduce-scatter.32
  459.5 31.1 reduce-scatter.34
  493.3 31.4 reduce-scatter.38
  527.3 31.3 reduce-scatter.40
  561.3 31.4 reduce-scatter.36
  631.5 13.0 all-gather.8
  712.7 27.7 reduce-scatter.28
  742.0 16.7 all-gather.12
  760.2 16.7 all-gather.10
  851.0 31.2 reduce-scatter.30
  886.5 17.3 all-gather.14
  968.6 31.7 reduce-scatter.32
  1046.4 31.1 reduce-scatter.34
  1080.0 31.4 reduce-scatter.38
  1114.2 31.4 reduce-scatter.40
  1148.2 31.4 reduce-scatter.36
Sparse Core Ops, SparseCore 1:
  1191.3 61.3 reduce-scatter.18
  1256.4 60.3 reduce-scatter.16
  1320.6 60.3 reduce-scatter.22
  1384.9 61.1 reduce-scatter.20
  1450.4 62.2 reduce-scatter.14
  1516.6 62.5 reduce-scatter.24
  1583.4 62.5 reduce-scatter.26
